TPU v7x, 256 devices: a whole 4x4x8 slice. The times are simulated.
256 devices in a mesh: row: 16 (over x, y_lo, core), col: 16 (over z, y_hi).
Axes of the slice: x: 4, y: 4 (y_hi: 2, y_lo: 2; y = y_hi * 2 + y_lo), z: 8, core: 2. Of those that a mesh axis runs over, the one named last changes fastest.
Arguments:
- ancestor_inverse: float32 [24576, 24576], P('row', 'col'), may hold values from -1 to 5, as said below
- factor_panel: float32 [24576, 512], P('row'), may hold values from -6 to 6
- ancestor_blocks: int32 [16, 12], replicated, may hold values from 0 to 11, each once within a row
- ancestor_count: int32 [16], replicated, may hold values from 1 to 12, 128 in all
Outputs:
- inverse_panel: float32 [24576, 512], P(('row', 'col'))
- inverse_row: float32 [512, 24576], P('row', 'col')
Inputs may be any that keep to these rules, and one draw needn't show every extreme that they name: ancestor_inverse is symmetric: equal to its transpose. `ancestor_blocks`: each row is an ordering of the 12 blocks of one tile. `ancestor_count`: the counts sum to 128, and some tile has all 12 slots live.
All inputs are finite; a program needn't handle non-finite values.
Results may differ from a plain program's by a relative error of at most 0.000071.
Values sent between devices are 32-bit elements; how exact they have to be, the bound alone decides.
No kernel may reach another device: no remote copies, remote signals or barrier semaphores. Data moves between devices by JAX's collectives and lax.ppermute only.
A program may use at most 128 MiB of HBM per device.

v0:
```python
import functools

import jax
import jax.numpy as jnp
from jax import lax
from jax.experimental import pallas as pl
from jax.experimental.pallas import tpu as pltpu
from jax.sharding import PartitionSpec as P


RING = 4
PIECES = 2
ORDER = (2, 1, 3, 0)


def emit_chunk(blocks_count, chunk, a, f_high, f_low, acc, keep_ref, send_ref):
    block, count = blocks_count
    share = keep_ref.shape[1]
    rows = acc.shape[0]
    dims = (((0,), (0,)), ((), ()))

    def product(left, right):
        return lax.dot_general(left, right, dims, preferred_element_type=jnp.float32)

    high = a.astype(jnp.bfloat16)
    low = (a - high.astype(jnp.float32)).astype(jnp.bfloat16)
    total = product(low, f_high[...]) + product(high, f_low[...]) + product(high, f_high[...])
    slot = chunk * (rows // block) + lax.broadcasted_iota(jnp.int32, (rows, 1), 0) // block
    acc[...] = jnp.where(slot < count, total, 0.0)
    r = lax.axis_index("row")
    core, y = r % 2, (r // 2) % 2
    for other in range(2):
        pair = 2 * jnp.where(other == 0, y, 1 - y)
        keep_ref[other] = acc[pl.ds((pair + core) * share, share), :]
        send_ref[other] = acc[pl.ds((pair + 1 - core) * share, share), :]


def column_copies(ahead, blocks, a_hbm, target, sems):
    tile_rows, chunk_rows = target.shape
    slots = blocks.shape[1]
    block = tile_rows // slots
    per_chunk = chunk_rows // block
    chunk = (lax.axis_index("row") // 4 + ahead) % RING
    copies = []
    for i in range(per_chunk):
        start = pl.multiple_of(blocks[lax.axis_index("col"), chunk * per_chunk + i] * block, block)
        copies.append(
            pltpu.make_async_copy(
                a_hbm.at[:, pl.ds(start, block)], target.at[:, pl.ds(i * block, block)], sems.at[i]
            )
        )
    return copies


def first_kernel(blocks_hbm, counts_hbm, a_hbm, f_hbm, keep_ref, send_ref, a_1, a_2, a_3, f_high, f_low, *scratch):
    a_buf, f_buf, acc, blocks, counts, a_sems, f_sems, table_sems = scratch
    slots = f_sems.shape[0]
    tile_rows = f_buf.shape[0]
    block = tile_rows // slots
    r, c = lax.axis_index("row"), lax.axis_index("col")
    tables = [
        pltpu.make_async_copy(blocks_hbm, blocks, table_sems.at[0]),
        pltpu.make_async_copy(counts_hbm, counts, table_sems.at[1]),
    ]
    for copy in tables:
        copy.start()

    def f_copy(s):
        span = pl.ds(pl.multiple_of(s * block, block), block)
        return pltpu.make_async_copy(f_hbm.at[span, :], f_buf.at[span, :], f_sems.at[s])

    for s in range(slots):
        f_copy(s).start()
    for copy in tables:
        copy.wait()
    now, *later = [
        column_copies(ahead, blocks, a_hbm, target, a_sems.at[i])
        for i, (ahead, target) in enumerate(zip(ORDER, (a_buf, a_1, a_2, a_3)))
    ]
    for copies in (now, *later):
        for copy in copies:
            copy.start()
    own_count = counts[r]

    @pl.loop(0, slots)
    def _(s):
        f_copy(s).wait()
        rows = f_buf[pl.ds(pl.multiple_of(s * block, block), block), :]
        rows = jnp.where(s < own_count, -rows, 0.0)
        high = rows.astype(jnp.bfloat16)
        target = pl.ds(pl.multiple_of(blocks[r, s] * block, block), block)
        f_high[target, :] = high
        f_low[target, :] = (rows - high.astype(jnp.float32)).astype(jnp.bfloat16)

    for copy in now:
        copy.wait()
    chunk = (r // 4 + ORDER[0]) % RING
    emit_chunk((block, counts[c]), chunk, a_buf[...], f_high, f_low, acc, keep_ref, send_ref)
    for copies in later:
        for copy in copies:
            copy.wait()


def next_kernel(step, slots, counts, a_now, f_high, f_low, keep_ref, send_ref, acc):
    block = a_now.shape[0] // slots
    chunk = (lax.axis_index("row") // 4 + ORDER[step]) % RING
    emit_chunk((block, counts[lax.axis_index("col")]), chunk, a_now[...], f_high, f_low, acc, keep_ref, send_ref)


SMEM = pl.BlockSpec(memory_space=pltpu.SMEM)
VMEM = pl.BlockSpec(memory_space=pltpu.VMEM)
HBM = pl.BlockSpec(memory_space=pltpu.HBM)
PARAMS = pltpu.CompilerParams(vmem_limit_bytes=24 * 1024 * 1024)


def chunk_products(blocks, counts, a, f, share):
    tile_rows, width = f.shape
    slots = blocks.shape[1]
    chunk_rows = tile_rows // RING
    per_chunk = slots // RING
    half = jax.ShapeDtypeStruct((2, share, width), jnp.float32)
    split = jax.ShapeDtypeStruct((tile_rows, width), jnp.bfloat16)
    columns = jax.ShapeDtypeStruct((tile_rows, chunk_rows), jnp.float32)
    acc = pltpu.VMEM((chunk_rows, width), jnp.float32)
    in_hbm = [pltpu.with_memory_space_constraint(value, pltpu.HBM) for value in (blocks, counts, a, f)]
    keep, send, *columns_of, high, low = pl.pallas_call(
        first_kernel,
        out_shape=(half, half, columns, columns, columns, split, split),
        in_specs=[HBM] * 4,
        out_specs=(VMEM,) * 7,
        scratch_shapes=[
            pltpu.VMEM((tile_rows, chunk_rows), jnp.float32),
            pltpu.VMEM((tile_rows, width), jnp.float32),
            acc,
            pltpu.SMEM(blocks.shape, jnp.int32),
            pltpu.SMEM(counts.shape, jnp.int32),
            pltpu.SemaphoreType.DMA((RING, per_chunk)),
            pltpu.SemaphoreType.DMA((slots,)),
            pltpu.SemaphoreType.DMA((2,)),
        ],
        compiler_params=PARAMS,
        name="product_0",
    )(*in_hbm)
    yield keep, send
    for step in range(1, RING):
        yield pl.pallas_call(
            functools.partial(next_kernel, step, slots),
            out_shape=(half, half),
            in_specs=[SMEM, VMEM, VMEM, VMEM],
            out_specs=(VMEM, VMEM),
            scratch_shapes=[acc],
            compiler_params=PARAMS,
        )(counts, columns_of[step - 1], high, low)


def per_device(ancestor_inverse, factor_panel, ancestor_blocks, ancestor_count):
    rows, cols = lax.axis_size("row"), lax.axis_size("col")
    width = factor_panel.shape[1]
    share_rows = factor_panel.shape[0] // rows
    piece = width // PIECES
    along_x = rows // RING

    def to(value, target):
        return lax.ppermute(value, "row", [(i, target(i)) for i in range(rows)])

    def ahead(value):
        return to(value, lambda i: (i + along_x) % rows)

    def behind(value):
        return to(value, lambda i: (i - along_x) % rows)

    products = list(chunk_products(ancestor_blocks, ancestor_count, ancestor_inverse, factor_panel, share_rows))
    far, front, back, own = [keep + to(send, lambda i: i ^ 1) for keep, send in products]
    from_back, from_front = ahead(far[0]), behind(far[1])
    swap = [(i * cols + j, j * cols + i) for i in range(rows) for j in range(cols)]
    arrivals = []
    for p in range(PIECES):
        part = slice(p * piece, (p + 1) * piece)
        plus = jnp.stack([front[0, :, part] + from_back[:, part], front[1, :, part]])
        minus = jnp.stack([back[0, :, part], back[1, :, part] + from_front[:, part]])
        front, back, plus, minus = lax.optimization_barrier((front, back, plus, minus))
        arrivals.append((own[:, :, part], ahead(plus), behind(minus)))
    halves = []
    for p in range(PIECES):
        total = sum(arrivals[p])
        if p + 1 < PIECES:
            total, arrivals[p + 1] = lax.optimization_barrier((total, (arrivals[p + 1][0],))), arrivals[p + 1]
            total, (following,) = total
            arrivals[p + 1] = (following,) + arrivals[p + 1][1:]
        halves.append((total[0], to(total[1], lambda i: i ^ 2)))
    shares, panels = [], []
    for p in range(PIECES):
        mine, other = halves[p]
        share = mine + other
        if p + 1 < PIECES:
            share, following = lax.optimization_barrier((share, halves[p + 1][0]))
            halves[p + 1] = (following, halves[p + 1][1])
        shares.append(share)
        panels.append(lax.ppermute(share, ("row", "col"), swap))
    share = jnp.concatenate(shares, axis=1)
    features = share.T.reshape(rows, width // rows, share_rows)
    mirrored = lax.all_to_all(features, "row", 0, 2, tiled=True)
    return jnp.concatenate(panels, axis=1), mirrored.reshape(width // rows, rows * share_rows)


def solution(mesh):
    return jax.shard_map(
        per_device,
        mesh=mesh,
        in_specs=(P("row", "col"), P("row", None), P(), P()),
        out_specs=(P(("row", "col"), None), P("row", "col")),
        check_vma=False,
    )
```

profile of v0, /device:TPU:137, one launch (start us, length us, event | category | flops | bytes accessed | tf_op | source)
XLA Modules:
  0.0 68.3 jit_solution(4108460725200782357)
XLA Ops:
  0.6 5.2 %product_0.1 = (f32[2,96,512]{2,1,0:T(8,128)S(1)}, f32[2,96,512]{2,1,0:T(8,128)S(1)}, f32[1536,384]{1,0:T(8,128)S(1)}, f32[1536,384]{1,0:T(8,128)S(1)}, f32[1536...) custom-call(s32[16,12]{1,0:T(8,128)} %blocks_hbm.1, s32[16]{0:T(128)} %counts.5, ...), custom_call_target="tpu_custom_call" | custom-call | tf_op jit(solution)/shard_map/product_0/pallas_call | solution.py:126
  5.8 0.8 %collective-permute-start.3 = (f32[2,96,512]{2,1,0:T(8,128)S(1)}, f32[2,96,512]{2,1,0:T(8,128)S(1)}, u32[]{:S(2)}, u32[]{:S(2)}) collective-permute-start(f32[2,96,512]{2,1,0:T(8,128)S(1)} %get-tuple-element.37), channel_id=1, source_target_pairs={{0,16},{16,0},{32,48},{48,32},{64,80},{80,64},{96,112},{112,96},{1... | collective-permute-start | bytes 1179656 | tf_op jit(solution)/shard_map/ppermute | solution.py:164
  6.6 2.6 %shard_map.59 = (f32[2,96,512]{2,1,0:T(8,128)S(1)}, f32[2,96,512]{2,1,0:T(8,128)S(1)}) custom-call(s32[16]{0:T(128)S(1)} %copy-done, f32[1536,384]{1,0:T(8,128)S(1)} %get-tuple-element.25.a_now, bf16[1536,512]{1,0:T(8,128)(2,1)S(1)} %get-tuple-element.26.f_high, bf16[1536,512]{1,0:T(8,128)(2,1)S(1)} %get-tuple-element.27.f_low), custom_call_target="tpu_custom_call" | custom-call | tf_op jit(solution)/shard_map/pallas_call | solution.py:146
  9.2 0.1 collective-permute-start
  9.3 2.6 %shard_map.60 = (f32[2,96,512]{2,1,0:T(8,128)S(1)}, f32[2,96,512]{2,1,0:T(8,128)S(1)}) custom-call(s32[16]{0:T(128)S(1)} %copy-done, f32[1536,384]{1,0:T(8,128)S(1)} %get-tuple-element.30.a_now, bf16[1536,512]{1,0:T(8,128)(2,1)S(1)} %get-tuple-element.26.f_high, bf16[1536,512]{1,0:T(8,128)(2,1)S(1)} %get-tuple-element.27.f_low), custom_call_target="tpu_custom_call" | custom-call | tf_op jit(solution)/shard_map/pallas_call | solution.py:146
  11.9 0.6 collective-permute-start.1
  12.5 2.6 %shard_map.61 = (f32[2,96,512]{2,1,0:T(8,128)S(1)}, f32[2,96,512]{2,1,0:T(8,128)S(1)}) custom-call(s32[16]{0:T(128)S(1)} %copy-done, f32[1536,384]{1,0:T(8,128)S(1)} %get-tuple-element.33.a_now, bf16[1536,512]{1,0:T(8,128)(2,1)S(1)} %get-tuple-element.26.f_high, bf16[1536,512]{1,0:T(8,128)(2,1)S(1)} %get-tuple-element.27.f_low), custom_call_target="tpu_custom_call" | custom-call | tf_op jit(solution)/shard_map/pallas_call | solution.py:146
  15.1 0.1 collective-permute-start.2
  15.2 0.1 add.45
  15.3 1.3 %collective-permute-start.4 = (f32[96,512]{1,0:T(8,128)S(1)}, f32[96,512]{1,0:T(8,128)S(1)}, u32[]{:S(2)}, u32[]{:S(2)}) collective-permute-start(f32[96,512]{1,0:T(8,128)S(1)} %get-tuple-element.51), channel_id=1, source_target_pairs={{0,64},{16,80},{32,96},{48,112},{64,128},{80,144},{96,160},{112,17... | collective-permute-start | bytes 589832 | tf_op jit(solution)/shard_map/ppermute | solution.py:164
  16.6 1.5 %collective-permute-start.5 = (f32[96,512]{1,0:T(8,128)S(1)}, f32[96,512]{1,0:T(8,128)S(1)}, u32[]{:S(2)}, u32[]{:S(2)}) collective-permute-start(f32[96,512]{1,0:T(8,128)S(1)} %get-tuple-element.50), channel_id=1, source_target_pairs={{0,192},{16,208},{32,224},{48,240},{64,0},{80,16},{96,32},{112,48}... | collective-permute-start | bytes 589832 | tf_op jit(solution)/shard_map/ppermute | solution.py:164
  18.1 0.1 add.43
  18.2 0.1 add.44
  18.3 0.1 add.42
  18.3 4.3 %collective-permute-done.4 = f32[96,512]{1,0:T(8,128)S(1)} collective-permute-done((f32[96,512]{1,0:T(8,128)S(1)}, f32[96,512]{1,0:T(8,128)S(1)}, u32[]{:S(2)}, u32[]{:S(2)}) %collective-permute-start.4) | collective-permute-done | bytes 196640 | tf_op jit(solution)/shard_map/ppermute | solution.py:164
  22.7 1.0 %collective-permute-start.6 = (f32[2,96,256]{2,1,0:T(8,128)S(1)}, f32[2,96,256]{2,1,0:T(8,128)S(1)}, u32[]{:S(2)}, u32[]{:S(2)}) collective-permute-start(f32[2,96,256]{2,1,0:T(8,128)S(1)} %pad_maximum_fusion), channel_id=1, source_target_pairs={{0,64},{16,80},{32,96},{48,112},{64,128},{80,144},{96,160},{112,17... | collective-permute-start | bytes 589832 | tf_op jit(solution)/shard_map/ppermute | solution.py:164
  23.7 1.8 %collective-permute-start.7 = (f32[2,96,256]{2,1,0:T(8,128)S(1)}, f32[2,96,256]{2,1,0:T(8,128)S(1)}, u32[]{:S(2)}, u32[]{:S(2)}) collective-permute-start(f32[2,96,256]{2,1,0:T(8,128)S(1)} %pad_maximum_fusion.1), channel_id=1, source_target_pairs={{0,192},{16,208},{32,224},{48,240},{64,0},{80,16},{96,32},{112,48}... | collective-permute-start | bytes 589832 | tf_op jit(solution)/shard_map/ppermute | solution.py:164
  25.6 0.3 collective-permute-start.9
  25.8 2.7 %collective-permute-start.10 = (f32[2,96,256]{2,1,0:T(8,128)S(1)}, f32[2,96,256]{2,1,0:T(8,128)S(1)}, u32[]{:S(2)}, u32[]{:S(2)}) collective-permute-start(f32[2,96,256]{2,1,0:T(8,128)S(1)} %pad_maximum_fusion.3), channel_id=1, source_target_pairs={{0,192},{16,208},{32,224},{48,240},{64,0},{80,16},{96,32},{112,48}... | collective-permute-start | bytes 589832 | tf_op jit(solution)/shard_map/ppermute | solution.py:164
  28.5 0.6 collective-permute-done.6
  29.2 0.3 collective-permute-start.8
  29.5 4.5 %collective-permute-done.9 = f32[2,96,256]{2,1,0:T(8,128)S(1)} collective-permute-done((f32[2,96,256]{2,1,0:T(8,128)S(1)}, f32[2,96,256]{2,1,0:T(8,128)S(1)}, u32[]{:S(2)}, u32[]{:S(2)}) %collective-permute-start.9) | collective-permute-done | bytes 196640 | tf_op jit(solution)/shard_map/ppermute | solution.py:164
  34.0 0.3 collective-permute-start.12
  34.3 7.7 %collective-permute-start.11 = (f32[96,256]{1,0:T(8,128)S(1)}, f32[96,256]{1,0:T(8,128)S(1)}, u32[]{:S(2)}, u32[]{:S(2)}) collective-permute-start(f32[96,256]{1,0:T(8,128)S(1)} %bitcast_add_fusion), channel_id=1, source_target_pairs={{0,0},{1,16},{2,32},{3,48},{4,64},{5,80},{6,96},{7,112},{8,128},{9... | collective-permute-start | bytes 294920 | tf_op jit(solution)/shard_map/ppermute | solution.py:199
  42.0 4.2 %collective-permute-start.13 = (f32[96,256]{1,0:T(8,128)S(1)}, f32[96,256]{1,0:T(8,128)S(1)}, u32[]{:S(2)}, u32[]{:S(2)}) collective-permute-start(f32[96,256]{1,0:T(8,128)S(1)} %add.55), channel_id=1, source_target_pairs={{0,0},{1,16},{2,32},{3,48},{4,64},{5,80},{6,96},{7,112},{8,128},{9... | collective-permute-start | bytes 294920 | tf_op jit(solution)/shard_map/ppermute | solution.py:199
  46.2 0.8 %copy.8 = f32[512,96]{1,0:T(8,128)} copy(f32[512,96]{0,1:T(8,128)S(1)} %maximum_bitcast_fusion) | data formatting | bytes 393216 | tf_op jit(solution)/shard_map/transpose | solution.py:201
  47.1 8.2 %all-to-all-start = ((f32[16,32,96]{2,1,0:T(8,128)}), f32[16,32,96]{2,1,0:T(8,128)S(1)}, u32[]{:S(2)}, u32[]{:S(2)}) async-start(f32[16,32,96]{2,1,0:T(8,128)} %bitcast.15), calls=%async_computation | async-start | bytes 524288 | tf_op jit(solution)/shard_map/all_to_all | solution.py:202
  55.3 3.3 %collective-permute-done.13 = f32[96,256]{1,0:T(8,128)S(1)} collective-permute-done((f32[96,256]{1,0:T(8,128)S(1)}, f32[96,256]{1,0:T(8,128)S(1)}, u32[]{:S(2)}, u32[]{:S(2)}) %collective-permute-start.13) | collective-permute-done | bytes 98336 | tf_op jit(solution)/shard_map/ppermute | solution.py:199
  58.6 0.7 %pad_maximum_fusion.4 = f32[96,512]{1,0:T(8,128)} fusion(f32[96,256]{1,0:T(8,128)S(1)} %collective-permute-done.13, f32[96,256]{1,0:T(8,128)S(1)} %collective-permute-done.11), kind=kLoop, calls=%fused_computation.8 | loop fusion | flops 49152 | bytes 393216 | tf_op jit(solution)/shard_map/concatenate | solution.py:203
  59.3 8.1 %all-to-all-done = f32[16,32,96]{2,1,0:T(8,128)S(1)} async-done(((f32[16,32,96]{2,1,0:T(8,128)}), f32[16,32,96]{2,1,0:T(8,128)S(1)}, u32[]{:S(2)}, u32[]{:S(2)}) %all-to-all-start) | async-done | bytes 196640 | tf_op jit(solution)/shard_map/all_to_all | solution.py:202
  67.4 0.2 copy.9
  67.5 0.8 %reshape.12 = f32[32,1536]{1,0:T(8,128)} reshape(f32[1,32,16,96]{3,2,1,0:T(8,128)S(1)} %copy.9) | data formatting | bytes 393216 | tf_op jit(solution)/shard_map/reshape | solution.py:203
  (31 shorter events, 0.4 us)
Async XLA Ops:
  0.6 6.0 %copy-start = (s32[16]{0:T(128)S(1)}, s32[16]{0:T(128)}, u32[]{:S(2)}) copy-start(s32[16]{0:T(128)} %counts.5) | copy-start | bytes 196
  5.8 9.4 %collective-permute-start.3 = (f32[2,96,512]{2,1,0:T(8,128)S(1)}, f32[2,96,512]{2,1,0:T(8,128)S(1)}, u32[]{:S(2)}, u32[]{:S(2)}) collective-permute-start(f32[2,96,512]{2,1,0:T(8,128)S(1)} %get-tuple-element.37), channel_id=1, source_target_pairs={{0,16},{16,0},{32,48},{48,32},{64,80},{80,64},{96,112},{112,96},{1... | collective-permute-start | bytes 1179656 | tf_op jit(solution)/shard_map/ppermute | solution.py:164
  9.2 9.1 %collective-permute-start = (f32[2,96,512]{2,1,0:T(8,128)S(1)}, f32[2,96,512]{2,1,0:T(8,128)S(1)}, u32[]{:S(2)}, u32[]{:S(2)}) collective-permute-start(f32[2,96,512]{2,1,0:T(8,128)S(1)} %get-tuple-element.29), channel_id=1, source_target_pairs={{0,16},{16,0},{32,48},{48,32},{64,80},{80,64},{96,112},{112,96},{1... | collective-permute-start | bytes 1179656 | tf_op jit(solution)/shard_map/ppermute | solution.py:164
  11.9 6.2 %collective-permute-start.1 = (f32[2,96,512]{2,1,0:T(8,128)S(1)}, f32[2,96,512]{2,1,0:T(8,128)S(1)}, u32[]{:S(2)}, u32[]{:S(2)}) collective-permute-start(f32[2,96,512]{2,1,0:T(8,128)S(1)} %get-tuple-element.32), channel_id=1, source_target_pairs={{0,16},{16,0},{32,48},{48,32},{64,80},{80,64},{96,112},{112,96},{1... | collective-permute-start | bytes 1179656 | tf_op jit(solution)/shard_map/ppermute | solution.py:164
  15.1 3.0 %collective-permute-start.2 = (f32[2,96,512]{2,1,0:T(8,128)S(1)}, f32[2,96,512]{2,1,0:T(8,128)S(1)}, u32[]{:S(2)}, u32[]{:S(2)}) collective-permute-start(f32[2,96,512]{2,1,0:T(8,128)S(1)} %get-tuple-element.35), channel_id=1, source_target_pairs={{0,16},{16,0},{32,48},{48,32},{64,80},{80,64},{96,112},{112,96},{1... | collective-permute-start | bytes 1179656 | tf_op jit(solution)/shard_map/ppermute | solution.py:164
  15.3 7.3 %collective-permute-start.4 = (f32[96,512]{1,0:T(8,128)S(1)}, f32[96,512]{1,0:T(8,128)S(1)}, u32[]{:S(2)}, u32[]{:S(2)}) collective-permute-start(f32[96,512]{1,0:T(8,128)S(1)} %get-tuple-element.51), channel_id=1, source_target_pairs={{0,64},{16,80},{32,96},{48,112},{64,128},{80,144},{96,160},{112,17... | collective-permute-start | bytes 589832 | tf_op jit(solution)/shard_map/ppermute | solution.py:164
  16.6 6.0 %collective-permute-start.5 = (f32[96,512]{1,0:T(8,128)S(1)}, f32[96,512]{1,0:T(8,128)S(1)}, u32[]{:S(2)}, u32[]{:S(2)}) collective-permute-start(f32[96,512]{1,0:T(8,128)S(1)} %get-tuple-element.50), channel_id=1, source_target_pairs={{0,192},{16,208},{32,224},{48,240},{64,0},{80,16},{96,32},{112,48}... | collective-permute-start | bytes 589832 | tf_op jit(solution)/shard_map/ppermute | solution.py:164
  22.7 6.4 %collective-permute-start.6 = (f32[2,96,256]{2,1,0:T(8,128)S(1)}, f32[2,96,256]{2,1,0:T(8,128)S(1)}, u32[]{:S(2)}, u32[]{:S(2)}) collective-permute-start(f32[2,96,256]{2,1,0:T(8,128)S(1)} %pad_maximum_fusion), channel_id=1, source_target_pairs={{0,64},{16,80},{32,96},{48,112},{64,128},{80,144},{96,160},{112,17... | collective-permute-start | bytes 589832 | tf_op jit(solution)/shard_map/ppermute | solution.py:164
  23.7 5.5 %collective-permute-start.7 = (f32[2,96,256]{2,1,0:T(8,128)S(1)}, f32[2,96,256]{2,1,0:T(8,128)S(1)}, u32[]{:S(2)}, u32[]{:S(2)}) collective-permute-start(f32[2,96,256]{2,1,0:T(8,128)S(1)} %pad_maximum_fusion.1), channel_id=1, source_target_pairs={{0,192},{16,208},{32,224},{48,240},{64,0},{80,16},{96,32},{112,48}... | collective-permute-start | bytes 589832 | tf_op jit(solution)/shard_map/ppermute | solution.py:164
  25.6 8.4 %collective-permute-start.9 = (f32[2,96,256]{2,1,0:T(8,128)S(1)}, f32[2,96,256]{2,1,0:T(8,128)S(1)}, u32[]{:S(2)}, u32[]{:S(2)}) collective-permute-start(f32[2,96,256]{2,1,0:T(8,128)S(1)} %pad_maximum_fusion.2), channel_id=1, source_target_pairs={{0,64},{16,80},{32,96},{48,112},{64,128},{80,144},{96,160},{112,17... | collective-permute-start | bytes 589832 | tf_op jit(solution)/shard_map/ppermute | solution.py:164
  25.8 8.1 %collective-permute-start.10 = (f32[2,96,256]{2,1,0:T(8,128)S(1)}, f32[2,96,256]{2,1,0:T(8,128)S(1)}, u32[]{:S(2)}, u32[]{:S(2)}) collective-permute-start(f32[2,96,256]{2,1,0:T(8,128)S(1)} %pad_maximum_fusion.3), channel_id=1, source_target_pairs={{0,192},{16,208},{32,224},{48,240},{64,0},{80,16},{96,32},{112,48}... | collective-permute-start | bytes 589832 | tf_op jit(solution)/shard_map/ppermute | solution.py:164
  29.2 5.1 %collective-permute-start.8 = (f32[96,256]{1,0:T(8,128)S(1)}, f32[96,256]{1,0:T(8,128)S(1)}, u32[]{:S(2)}, u32[]{:S(2)}) collective-permute-start(f32[96,256]{1,0:T(8,128)S(1)} %slice_bitcast_fusion.6), channel_id=1, source_target_pairs={{0,32},{16,48},{32,0},{48,16},{64,96},{80,112},{96,64},{112,80},{1... | collective-permute-start | bytes 294920 | tf_op jit(solution)/shard_map/ppermute | solution.py:164
  34.0 8.0 %collective-permute-start.12 = (f32[96,256]{1,0:T(8,128)S(1)}, f32[96,256]{1,0:T(8,128)S(1)}, u32[]{:S(2)}, u32[]{:S(2)}) collective-permute-start(f32[96,256]{1,0:T(8,128)S(1)} %get-tuple-element.52), channel_id=1, source_target_pairs={{0,32},{16,48},{32,0},{48,16},{64,96},{80,112},{96,64},{112,80},{1... | collective-permute-start | bytes 294920 | tf_op jit(solution)/shard_map/ppermute | solution.py:164
  34.3 21.0 %collective-permute-start.11 = (f32[96,256]{1,0:T(8,128)S(1)}, f32[96,256]{1,0:T(8,128)S(1)}, u32[]{:S(2)}, u32[]{:S(2)}) collective-permute-start(f32[96,256]{1,0:T(8,128)S(1)} %bitcast_add_fusion), channel_id=1, source_target_pairs={{0,0},{1,16},{2,32},{3,48},{4,64},{5,80},{6,96},{7,112},{8,128},{9... | collective-permute-start | bytes 294920 | tf_op jit(solution)/shard_map/ppermute | solution.py:199
  42.0 16.5 %collective-permute-start.13 = (f32[96,256]{1,0:T(8,128)S(1)}, f32[96,256]{1,0:T(8,128)S(1)}, u32[]{:S(2)}, u32[]{:S(2)}) collective-permute-start(f32[96,256]{1,0:T(8,128)S(1)} %add.55), channel_id=1, source_target_pairs={{0,0},{1,16},{2,32},{3,48},{4,64},{5,80},{6,96},{7,112},{8,128},{9... | collective-permute-start | bytes 294920 | tf_op jit(solution)/shard_map/ppermute | solution.py:199
  47.1 20.3 %all-to-all-start = ((f32[16,32,96]{2,1,0:T(8,128)}), f32[16,32,96]{2,1,0:T(8,128)S(1)}, u32[]{:S(2)}, u32[]{:S(2)}) async-start(f32[16,32,96]{2,1,0:T(8,128)} %bitcast.15), calls=%async_computation | async-start | bytes 524288 | tf_op jit(solution)/shard_map/all_to_all | solution.py:202
where the time goes:
time: 68.6 us; the launch traced here: 68.3 us
  starting transfers between devices  30.6 us (45%)
  waiting for transfers between devices  20.8 us (30%)
  Pallas kernels  13 us (19%)
  local copies, waits for them, and re-layouts  1.91 us (3%)
  other arithmetic  1.18 us (2%)
  between operations  0.89 us (1%)
    ppermute x2, starting transfers between devices, per_device(): panels.append(lax.ppermute(share, ('row', 'col'), swap))  11.9 us
    ppermute x12, starting transfers between devices, to(): return lax.ppermute(value, 'row', [(i, target(i)) for i in range(rows)])  10.5 us
    ppermute x12, waiting for transfers between devices, to(): return lax.ppermute(value, 'row', [(i, target(i)) for i in range(rows)])  9.4 us
    all_to_all x1, starting transfers between devices, per_device(): mirrored = lax.all_to_all(features, 'row', 0, 2, tiled=True)  8.19 us
    all_to_all x1, waiting for transfers between devices, per_device(): mirrored = lax.all_to_all(features, 'row', 0, 2, tiled=True)  8.11 us
    pallas_call x3, Pallas kernels, chunk_products(): pl.pallas_call(functools.partial(next_kernel, step, slots), out_shape=(ha...  7.82 us
    pallas_call x1, Pallas kernels, chunk_products(): pl.pallas_call(first_kernel, out_shape=(half, half, columns, columns, col...  5.17 us
    ppermute x2, waiting for transfers between devices, per_device(): panels.append(lax.ppermute(share, ('row', 'col'), swap))  3.28 us
  transfers between devices with their start and end apart: 15, of which 5 were waited for; matrix products, arithmetic and copies ran while one was open for 3% of the time, Pallas kernels for 11%

commit v1 on v0

--- a/solution.py
+++ b/solution.py
@@ -11,6 +11,14 @@
 RING = 4
 PIECES = 2
 ORDER = (2, 1, 3, 0)
+
+
+def chunk_of(x, c):
+    return (2 * (c // RING) + 2 * RING + 2 - x) % RING
+
+
+def share_of(r, c):
+    return RING * chunk_of(r // RING, c) + 2 * (r % 2) + (r // 2) % 2
 
 
 def emit_chunk(blocks_count, chunk, a, f_high, f_low, acc, keep_ref, send_ref):
@@ -30,9 +38,9 @@
     r = lax.axis_index("row")
     core, y = r % 2, (r // 2) % 2
     for other in range(2):
-        pair = 2 * jnp.where(other == 0, y, 1 - y)
-        keep_ref[other] = acc[pl.ds((pair + core) * share, share), :]
-        send_ref[other] = acc[pl.ds((pair + 1 - core) * share, share), :]
+        along_y = y if other == 0 else 1 - y
+        keep_ref[other] = acc[pl.ds((2 * core + along_y) * share, share), :]
+        send_ref[other] = acc[pl.ds((2 * (1 - core) + along_y) * share, share), :]
 
 
 def column_copies(ahead, blocks, a_hbm, target, sems):
@@ -40,7 +48,7 @@
     slots = blocks.shape[1]
     block = tile_rows // slots
     per_chunk = chunk_rows // block
-    chunk = (lax.axis_index("row") // 4 + ahead) % RING
+    chunk = chunk_of(lax.axis_index("row") // 4 + ahead, lax.axis_index("col"))
     copies = []
     for i in range(per_chunk):
         start = pl.multiple_of(blocks[lax.axis_index("col"), chunk * per_chunk + i] * block, block)
@@ -94,7 +102,7 @@
 
     for copy in now:
         copy.wait()
-    chunk = (r // 4 + ORDER[0]) % RING
+    chunk = chunk_of(r // 4 + ORDER[0], c)
     emit_chunk((block, counts[c]), chunk, a_buf[...], f_high, f_low, acc, keep_ref, send_ref)
     for copies in later:
         for copy in copies:
@@ -103,8 +111,9 @@
 
 def next_kernel(step, slots, counts, a_now, f_high, f_low, keep_ref, send_ref, acc):
     block = a_now.shape[0] // slots
-    chunk = (lax.axis_index("row") // 4 + ORDER[step]) % RING
-    emit_chunk((block, counts[lax.axis_index("col")]), chunk, a_now[...], f_high, f_low, acc, keep_ref, send_ref)
+    c = lax.axis_index("col")
+    chunk = chunk_of(lax.axis_index("row") // 4 + ORDER[step], c)
+    emit_chunk((block, counts[c]), chunk, a_now[...], f_high, f_low, acc, keep_ref, send_ref)
 
 
 SMEM = pl.BlockSpec(memory_space=pltpu.SMEM)
@@ -172,7 +181,7 @@
     products = list(chunk_products(ancestor_blocks, ancestor_count, ancestor_inverse, factor_panel, share_rows))
     far, front, back, own = [keep + to(send, lambda i: i ^ 1) for keep, send in products]
     from_back, from_front = ahead(far[0]), behind(far[1])
-    swap = [(i * cols + j, j * cols + i) for i in range(rows) for j in range(cols)]
+    swap = [(i * cols + j, j * cols + share_of(i, j)) for i in range(rows) for j in range(cols)]
     arrivals = []
     for p in range(PIECES):
         part = slice(p * piece, (p + 1) * piece)
@@ -188,7 +197,7 @@
             total, (following,) = total
             arrivals[p + 1] = (following,) + arrivals[p + 1][1:]
         halves.append((total[0], to(total[1], lambda i: i ^ 2)))
-    shares, panels = [], []
+    shares = []
     for p in range(PIECES):
         mine, other = halves[p]
         share = mine + other
@@ -196,11 +205,33 @@
             share, following = lax.optimization_barrier((share, halves[p + 1][0]))
             halves[p + 1] = (following, halves[p + 1][1])
         shares.append(share)
-        panels.append(lax.ppermute(share, ("row", "col"), swap))
     share = jnp.concatenate(shares, axis=1)
+    inverse_panel = lax.ppermute(share, ("row", "col"), swap)
     features = share.T.reshape(rows, width // rows, share_rows)
-    mirrored = lax.all_to_all(features, "row", 0, 2, tiled=True)
-    return jnp.concatenate(panels, axis=1), mirrored.reshape(width // rows, rows * share_rows)
+    pieces = lax.all_to_all(features, "row", 0, 0, tiled=True)
+    return inverse_panel, in_order(pieces)
+
+
+def in_order_kernel(pieces, out):
+    rows = pieces.shape[0]
+    c = lax.axis_index("col")
+    parts = []
+    for s in range(rows):
+        x = (2 * (c // RING) + 2 * RING + 2 - s // RING) % RING
+        parts.append(pieces[RING * x + 2 * (s % 2) + (s // 2) % 2])
+    out[...] = jnp.concatenate(parts, axis=1)
+
+
+def in_order(pieces):
+    count, height, columns = pieces.shape
+    return pl.pallas_call(
+        in_order_kernel,
+        out_shape=jax.ShapeDtypeStruct((height, count * columns), pieces.dtype),
+        in_specs=[VMEM],
+        out_specs=VMEM,
+        compiler_params=pltpu.CompilerParams(vmem_limit_bytes=8 * 1024 * 1024),
+        name="in_order",
+    )(pieces)
 
 
 def solution(mesh):

time: 68.6 us -> 62.4 us (0.910)
  the two profiles are of different devices: /device:TPU:137 before, /device:TPU:1 now
where the time goes in v1:
time: 62.4 us; the launch traced here: 62.3 us
  starting transfers between devices  20.1 us (32%)
  Pallas kernels  13.8 us (22%)
  waiting for transfers between devices  13.1 us (21%)
  blocking collectives  13.1 us (21%)
  between operations  0.91 us (1%)
  local copies, waits for them, and re-layouts  0.89 us (1%)
    all_to_all x1, blocking collectives, per_device(): pieces = lax.all_to_all(features, 'row', 0, 0, tiled=True)  13.1 us
    ppermute x12, waiting for transfers between devices, to(): return lax.ppermute(value, 'row', [(i, target(i)) for i in range(rows)])  13.1 us
    ppermute x12, starting transfers between devices, to(): return lax.ppermute(value, 'row', [(i, target(i)) for i in range(rows)])  12.7 us
    pallas_call x3, Pallas kernels, chunk_products(): pl.pallas_call(functools.partial(next_kernel, step, slots), out_shape=(ha...  7.82 us
    ppermute x1, starting transfers between devices, per_device(): inverse_panel = lax.ppermute(share, ('row', 'col'), swap)  7.37 us
    pallas_call x1, Pallas kernels, chunk_products(): pl.pallas_call(first_kernel, out_shape=(half, half, columns, columns, col...  5.17 us
  transfers between devices with their start and end apart: 13, of which 4 were waited for; matrix products, arithmetic and copies ran while one was open for 1% of the time, Pallas kernels for 14%

profile of v1, /device:TPU:1, one launch (start us, length us, event | category | flops | bytes accessed | tf_op | source)
XLA Modules:
  0.0 62.3 jit_solution(192596787215992211)
XLA Ops:
  0.6 5.2 %product_0.1 = (f32[2,96,512]{2,1,0:T(8,128)S(1)}, f32[2,96,512]{2,1,0:T(8,128)S(1)}, f32[1536,384]{1,0:T(8,128)S(1)}, f32[1536,384]{1,0:T(8,128)S(1)}, f32[1536...) custom-call(s32[16,12]{1,0:T(8,128)} %blocks_hbm.1, s32[16]{0:T(128)} %counts.5, ...), custom_call_target="tpu_custom_call" | custom-call | tf_op jit(solution)/shard_map/product_0/pallas_call | solution.py:135
  5.8 3.3 %collective-permute-start.3 = (f32[2,96,512]{2,1,0:T(8,128)S(1)}, f32[2,96,512]{2,1,0:T(8,128)S(1)}, u32[]{:S(2)}, u32[]{:S(2)}) collective-permute-start(f32[2,96,512]{2,1,0:T(8,128)S(1)} %get-tuple-element.37), channel_id=1, source_target_pairs={{0,16},{16,0},{32,48},{48,32},{64,80},{80,64},{96,112},{112,96},{1... | collective-permute-start | bytes 1179656 | tf_op jit(solution)/shard_map/ppermute | solution.py:173
  9.1 2.6 %shard_map.59 = (f32[2,96,512]{2,1,0:T(8,128)S(1)}, f32[2,96,512]{2,1,0:T(8,128)S(1)}) custom-call(s32[16]{0:T(128)S(1)} %copy-done, f32[1536,384]{1,0:T(8,128)S(1)} %get-tuple-element.25.a_now, bf16[1536,512]{1,0:T(8,128)(2,1)S(1)} %get-tuple-element.26.f_high, bf16[1536,512]{1,0:T(8,128)(2,1)S(1)} %get-tuple-element.27.f_low), custom_call_target="tpu_custom_call" | custom-call | tf_op jit(solution)/shard_map/pallas_call | solution.py:155
  11.7 0.1 collective-permute-start
  11.8 2.6 %shard_map.60 = (f32[2,96,512]{2,1,0:T(8,128)S(1)}, f32[2,96,512]{2,1,0:T(8,128)S(1)}) custom-call(s32[16]{0:T(128)S(1)} %copy-done, f32[1536,384]{1,0:T(8,128)S(1)} %get-tuple-element.30.a_now, bf16[1536,512]{1,0:T(8,128)(2,1)S(1)} %get-tuple-element.26.f_high, bf16[1536,512]{1,0:T(8,128)(2,1)S(1)} %get-tuple-element.27.f_low), custom_call_target="tpu_custom_call" | custom-call | tf_op jit(solution)/shard_map/pallas_call | solution.py:155
  14.5 0.6 collective-permute-start.1
  15.0 2.6 %shard_map.61 = (f32[2,96,512]{2,1,0:T(8,128)S(1)}, f32[2,96,512]{2,1,0:T(8,128)S(1)}) custom-call(s32[16]{0:T(128)S(1)} %copy-done, f32[1536,384]{1,0:T(8,128)S(1)} %get-tuple-element.33.a_now, bf16[1536,512]{1,0:T(8,128)(2,1)S(1)} %get-tuple-element.26.f_high, bf16[1536,512]{1,0:T(8,128)(2,1)S(1)} %get-tuple-element.27.f_low), custom_call_target="tpu_custom_call" | custom-call | tf_op jit(solution)/shard_map/pallas_call | solution.py:155
  17.6 0.1 collective-permute-start.2
  17.8 0.1 add.45
  17.8 0.1 collective-permute-start.4
  17.9 2.7 %collective-permute-start.5 = (f32[96,512]{1,0:T(8,128)S(1)}, f32[96,512]{1,0:T(8,128)S(1)}, u32[]{:S(2)}, u32[]{:S(2)}) collective-permute-start(f32[96,512]{1,0:T(8,128)S(1)} %get-tuple-element.50), channel_id=1, source_target_pairs={{0,192},{16,208},{32,224},{48,240},{64,0},{80,16},{96,32},{112,48}... | collective-permute-start | bytes 589832 | tf_op jit(solution)/shard_map/ppermute | solution.py:173
  20.6 0.1 add.43
  20.7 0.1 add.44
  20.8 0.1 add.42
  20.8 4.3 %collective-permute-done.4 = f32[96,512]{1,0:T(8,128)S(1)} collective-permute-done((f32[96,512]{1,0:T(8,128)S(1)}, f32[96,512]{1,0:T(8,128)S(1)}, u32[]{:S(2)}, u32[]{:S(2)}) %collective-permute-start.4) | collective-permute-done | bytes 196640 | tf_op jit(solution)/shard_map/ppermute | solution.py:173
  25.2 0.1 collective-permute-start.6
  25.3 2.7 %collective-permute-start.7 = (f32[2,96,256]{2,1,0:T(8,128)S(1)}, f32[2,96,256]{2,1,0:T(8,128)S(1)}, u32[]{:S(2)}, u32[]{:S(2)}) collective-permute-start(f32[2,96,256]{2,1,0:T(8,128)S(1)} %pad_maximum_fusion.1), channel_id=1, source_target_pairs={{0,192},{16,208},{32,224},{48,240},{64,0},{80,16},{96,32},{112,48}... | collective-permute-start | bytes 589832 | tf_op jit(solution)/shard_map/ppermute | solution.py:173
  28.1 0.3 collective-permute-start.9
  28.4 2.7 %collective-permute-start.10 = (f32[2,96,256]{2,1,0:T(8,128)S(1)}, f32[2,96,256]{2,1,0:T(8,128)S(1)}, u32[]{:S(2)}, u32[]{:S(2)}) collective-permute-start(f32[2,96,256]{2,1,0:T(8,128)S(1)} %pad_maximum_fusion.3), channel_id=1, source_target_pairs={{0,192},{16,208},{32,224},{48,240},{64,0},{80,16},{96,32},{112,48}... | collective-permute-start | bytes 589832 | tf_op jit(solution)/shard_map/ppermute | solution.py:173
  31.0 0.6 %collective-permute-done.6 = f32[2,96,256]{2,1,0:T(8,128)S(1)} collective-permute-done((f32[2,96,256]{2,1,0:T(8,128)S(1)}, f32[2,96,256]{2,1,0:T(8,128)S(1)}, u32[]{:S(2)}, u32[]{:S(2)}) %collective-permute-start.6) | collective-permute-done | bytes 196640 | tf_op jit(solution)/shard_map/ppermute | solution.py:173
  31.7 0.0 collective-permute-done.7
  31.7 0.1 fusion.6
  31.7 0.1 collective-permute-start.8
  31.8 4.6 %collective-permute-done.9 = f32[2,96,256]{2,1,0:T(8,128)S(1)} collective-permute-done((f32[2,96,256]{2,1,0:T(8,128)S(1)}, f32[2,96,256]{2,1,0:T(8,128)S(1)}, u32[]{:S(2)}, u32[]{:S(2)}) %collective-permute-start.9) | collective-permute-done | bytes 196640 | tf_op jit(solution)/shard_map/ppermute | solution.py:173
  36.5 0.0 collective-permute-done.10
  36.5 0.1 collective-permute-start.11
  36.7 3.5 %collective-permute-done.11 = f32[96,256]{1,0:T(8,128)S(1)} collective-permute-done((f32[96,256]{1,0:T(8,128)S(1)}, f32[96,256]{1,0:T(8,128)S(1)}, u32[]{:S(2)}, u32[]{:S(2)}) %collective-permute-start.11) | collective-permute-done | bytes 98336 | tf_op jit(solution)/shard_map/ppermute | solution.py:173
  40.3 7.4 %collective-permute-start.12 = (f32[96,512]{1,0:T(8,128)S(1)}, f32[96,512]{1,0:T(8,128)S(1)}, u32[]{:S(2)}, u32[]{:S(2)}) collective-permute-start(f32[96,512]{1,0:T(8,128)S(1)} %get-tuple-element.53), channel_id=1, source_target_pairs={{0,8},{1,24},{2,40},{3,56},{4,64},{5,80},{6,96},{7,112},{8,136},{9... | collective-permute-start | bytes 589832 | tf_op jit(solution)/shard_map/ppermute | solution.py:209
  47.6 0.1 copy.6
  47.8 13.1 %all_to_all.5.pieces = f32[16,32,96]{2,1,0:T(8,128)S(1)} all-to-all(f32[16,32,96]{2,1,0:T(8,128)S(1)} %bitcast.35), channel_id=1, replica_groups=mesh['row'=16,'col'=16] {'row'}, dimensions={0} | all-to-all | bytes 393216 | tf_op jit(solution)/shard_map/all_to_all | solution.py:211
  60.9 0.8 %in_order.1 = f32[32,1536]{1,0:T(8,128)} custom-call(f32[16,32,96]{2,1,0:T(8,128)S(1)} %all_to_all.5.pieces), custom_call_target="tpu_custom_call" | custom-call | tf_op jit(solution)/shard_map/in_order/pallas_call | solution.py:227
  61.6 0.7 %copy.8 = f32[96,512]{1,0:T(8,128)} copy(f32[96,512]{1,0:T(8,128)S(1)} %collective-permute-done.12) | data formatting | bytes 393216
  (27 shorter events, 0.3 us)
Async XLA Ops:
  0.6 8.5 %copy-start = (s32[16]{0:T(128)S(1)}, s32[16]{0:T(128)}, u32[]{:S(2)}) copy-start(s32[16]{0:T(128)} %counts.5) | copy-start | bytes 196
  5.8 11.9 %collective-permute-start.3 = (f32[2,96,512]{2,1,0:T(8,128)S(1)}, f32[2,96,512]{2,1,0:T(8,128)S(1)}, u32[]{:S(2)}, u32[]{:S(2)}) collective-permute-start(f32[2,96,512]{2,1,0:T(8,128)S(1)} %get-tuple-element.37), channel_id=1, source_target_pairs={{0,16},{16,0},{32,48},{48,32},{64,80},{80,64},{96,112},{112,96},{1... | collective-permute-start | bytes 1179656 | tf_op jit(solution)/shard_map/ppermute | solution.py:173
  11.7 9.1 %collective-permute-start = (f32[2,96,512]{2,1,0:T(8,128)S(1)}, f32[2,96,512]{2,1,0:T(8,128)S(1)}, u32[]{:S(2)}, u32[]{:S(2)}) collective-permute-start(f32[2,96,512]{2,1,0:T(8,128)S(1)} %get-tuple-element.29), channel_id=1, source_target_pairs={{0,16},{16,0},{32,48},{48,32},{64,80},{80,64},{96,112},{112,96},{1... | collective-permute-start | bytes 1179656 | tf_op jit(solution)/shard_map/ppermute | solution.py:173
  14.5 6.2 %collective-permute-start.1 = (f32[2,96,512]{2,1,0:T(8,128)S(1)}, f32[2,96,512]{2,1,0:T(8,128)S(1)}, u32[]{:S(2)}, u32[]{:S(2)}) collective-permute-start(f32[2,96,512]{2,1,0:T(8,128)S(1)} %get-tuple-element.32), channel_id=1, source_target_pairs={{0,16},{16,0},{32,48},{48,32},{64,80},{80,64},{96,112},{112,96},{1... | collective-permute-start | bytes 1179656 | tf_op jit(solution)/shard_map/ppermute | solution.py:173
  17.6 3.0 %collective-permute-start.2 = (f32[2,96,512]{2,1,0:T(8,128)S(1)}, f32[2,96,512]{2,1,0:T(8,128)S(1)}, u32[]{:S(2)}, u32[]{:S(2)}) collective-permute-start(f32[2,96,512]{2,1,0:T(8,128)S(1)} %get-tuple-element.35), channel_id=1, source_target_pairs={{0,16},{16,0},{32,48},{48,32},{64,80},{80,64},{96,112},{112,96},{1... | collective-permute-start | bytes 1179656 | tf_op jit(solution)/shard_map/ppermute | solution.py:173
  17.8 7.3 %collective-permute-start.4 = (f32[96,512]{1,0:T(8,128)S(1)}, f32[96,512]{1,0:T(8,128)S(1)}, u32[]{:S(2)}, u32[]{:S(2)}) collective-permute-start(f32[96,512]{1,0:T(8,128)S(1)} %get-tuple-element.51), channel_id=1, source_target_pairs={{0,64},{16,80},{32,96},{48,112},{64,128},{80,144},{96,160},{112,17... | collective-permute-start | bytes 589832 | tf_op jit(solution)/shard_map/ppermute | solution.py:173
  17.9 7.2 %collective-permute-start.5 = (f32[96,512]{1,0:T(8,128)S(1)}, f32[96,512]{1,0:T(8,128)S(1)}, u32[]{:S(2)}, u32[]{:S(2)}) collective-permute-start(f32[96,512]{1,0:T(8,128)S(1)} %get-tuple-element.50), channel_id=1, source_target_pairs={{0,192},{16,208},{32,224},{48,240},{64,0},{80,16},{96,32},{112,48}... | collective-permute-start | bytes 589832 | tf_op jit(solution)/shard_map/ppermute | solution.py:173
  25.2 6.4 %collective-permute-start.6 = (f32[2,96,256]{2,1,0:T(8,128)S(1)}, f32[2,96,256]{2,1,0:T(8,128)S(1)}, u32[]{:S(2)}, u32[]{:S(2)}) collective-permute-start(f32[2,96,256]{2,1,0:T(8,128)S(1)} %pad_maximum_fusion), channel_id=1, source_target_pairs={{0,64},{16,80},{32,96},{48,112},{64,128},{80,144},{96,160},{112,17... | collective-permute-start | bytes 589832 | tf_op jit(solution)/shard_map/ppermute | solution.py:173
  25.3 6.3 %collective-permute-start.7 = (f32[2,96,256]{2,1,0:T(8,128)S(1)}, f32[2,96,256]{2,1,0:T(8,128)S(1)}, u32[]{:S(2)}, u32[]{:S(2)}) collective-permute-start(f32[2,96,256]{2,1,0:T(8,128)S(1)} %pad_maximum_fusion.1), channel_id=1, source_target_pairs={{0,192},{16,208},{32,224},{48,240},{64,0},{80,16},{96,32},{112,48}... | collective-permute-start | bytes 589832 | tf_op jit(solution)/shard_map/ppermute | solution.py:173
  28.1 8.4 %collective-permute-start.9 = (f32[2,96,256]{2,1,0:T(8,128)S(1)}, f32[2,96,256]{2,1,0:T(8,128)S(1)}, u32[]{:S(2)}, u32[]{:S(2)}) collective-permute-start(f32[2,96,256]{2,1,0:T(8,128)S(1)} %pad_maximum_fusion.2), channel_id=1, source_target_pairs={{0,64},{16,80},{32,96},{48,112},{64,128},{80,144},{96,160},{112,17... | collective-permute-start | bytes 589832 | tf_op jit(solution)/shard_map/ppermute | solution.py:173
  28.4 8.1 %collective-permute-start.10 = (f32[2,96,256]{2,1,0:T(8,128)S(1)}, f32[2,96,256]{2,1,0:T(8,128)S(1)}, u32[]{:S(2)}, u32[]{:S(2)}) collective-permute-start(f32[2,96,256]{2,1,0:T(8,128)S(1)} %pad_maximum_fusion.3), channel_id=1, source_target_pairs={{0,192},{16,208},{32,224},{48,240},{64,0},{80,16},{96,32},{112,48}... | collective-permute-start | bytes 589832 | tf_op jit(solution)/shard_map/ppermute | solution.py:173
  31.7 4.9 %collective-permute-start.8 = (f32[96,256]{1,0:T(8,128)S(1)}, f32[96,256]{1,0:T(8,128)S(1)}, u32[]{:S(2)}, u32[]{:S(2)}) collective-permute-start(f32[96,256]{1,0:T(8,128)S(1)} %slice_bitcast_fusion.6), channel_id=1, source_target_pairs={{0,32},{16,48},{32,0},{48,16},{64,96},{80,112},{96,64},{112,80},{1... | collective-permute-start | bytes 294920 | tf_op jit(solution)/shard_map/ppermute | solution.py:173
  36.5 3.7 %collective-permute-start.11 = (f32[96,256]{1,0:T(8,128)S(1)}, f32[96,256]{1,0:T(8,128)S(1)}, u32[]{:S(2)}, u32[]{:S(2)}) collective-permute-start(f32[96,256]{1,0:T(8,128)S(1)} %get-tuple-element.54), channel_id=1, source_target_pairs={{0,32},{16,48},{32,0},{48,16},{64,96},{80,112},{96,64},{112,80},{1... | collective-permute-start | bytes 294920 | tf_op jit(solution)/shard_map/ppermute | solution.py:173
  40.3 21.4 %collective-permute-start.12 = (f32[96,512]{1,0:T(8,128)S(1)}, f32[96,512]{1,0:T(8,128)S(1)}, u32[]{:S(2)}, u32[]{:S(2)}) collective-permute-start(f32[96,512]{1,0:T(8,128)S(1)} %get-tuple-element.53), channel_id=1, source_target_pairs={{0,8},{1,24},{2,40},{3,56},{4,64},{5,80},{6,96},{7,112},{8,136},{9... | collective-permute-start | bytes 589832 | tf_op jit(solution)/shard_map/ppermute | solution.py:209

commit v2 on v1

--- a/solution.py
+++ b/solution.py
@@ -9,7 +9,6 @@
 
 
 RING = 4
-PIECES = 2
 ORDER = (2, 1, 3, 0)
 
 
@@ -166,7 +165,6 @@
     rows, cols = lax.axis_size("row"), lax.axis_size("col")
     width = factor_panel.shape[1]
     share_rows = factor_panel.shape[0] // rows
-    piece = width // PIECES
     along_x = rows // RING
 
     def to(value, target):
@@ -179,33 +177,18 @@
         return to(value, lambda i: (i - along_x) % rows)
 
     products = list(chunk_products(ancestor_blocks, ancestor_count, ancestor_inverse, factor_panel, share_rows))
-    far, front, back, own = [keep + to(send, lambda i: i ^ 1) for keep, send in products]
-    from_back, from_front = ahead(far[0]), behind(far[1])
+
+    def plane_sum(keep, send):
+        chip = keep + to(send, lambda i: i ^ 1)
+        return chip[0] + to(chip[1], lambda i: i ^ 2)
+
+    far, front, back, own = [plane_sum(*product) for product in products]
+    half = width // 2
+    from_back, from_front = ahead(far[:, :half]), behind(far[:, half:])
+    plus = jnp.concatenate([front[:, :half] + from_back, front[:, half:]], axis=1)
+    minus = jnp.concatenate([back[:, :half], back[:, half:] + from_front], axis=1)
+    share = own + ahead(plus) + behind(minus)
     swap = [(i * cols + j, j * cols + share_of(i, j)) for i in range(rows) for j in range(cols)]
-    arrivals = []
-    for p in range(PIECES):
-        part = slice(p * piece, (p + 1) * piece)
-        plus = jnp.stack([front[0, :, part] + from_back[:, part], front[1, :, part]])
-        minus = jnp.stack([back[0, :, part], back[1, :, part] + from_front[:, part]])
-        front, back, plus, minus = lax.optimization_barrier((front, back, plus, minus))
-        arrivals.append((own[:, :, part], ahead(plus), behind(minus)))
-    halves = []
-    for p in range(PIECES):
-        total = sum(arrivals[p])
-        if p + 1 < PIECES:
-            total, arrivals[p + 1] = lax.optimization_barrier((total, (arrivals[p + 1][0],))), arrivals[p + 1]
-            total, (following,) = total
-            arrivals[p + 1] = (following,) + arrivals[p + 1][1:]
-        halves.append((total[0], to(total[1], lambda i: i ^ 2)))
-    shares = []
-    for p in range(PIECES):
-        mine, other = halves[p]
-        share = mine + other
-        if p + 1 < PIECES:
-            share, following = lax.optimization_barrier((share, halves[p + 1][0]))
-            halves[p + 1] = (following, halves[p + 1][1])
-        shares.append(share)
-    share = jnp.concatenate(shares, axis=1)
     inverse_panel = lax.ppermute(share, ("row", "col"), swap)
     features = share.T.reshape(rows, width // rows, share_rows)
     pieces = lax.all_to_all(features, "row", 0, 0, tiled=True)

time: 62.4 us -> 65.1 us (1.043)
  waiting for transfers between devices: 13.1 us -> 16 us
    ppermute x12, waiting for transfers between devices: 13.1 us -> 16 us  [to(): return lax.ppermute(value, 'row', [(i, target(i)) for i in range(rows)])]
  transfers between devices with their start and end apart: 13 -> 13, of which waited for: 4 -> 4; matrix products, arithmetic and copies ran while one was open for 1% -> 1% of each run, Pallas kernels for 14% -> 9%
where the time goes in v2:
time: 65.1 us; the launch traced here: 64.9 us
  starting transfers between devices  19.9 us (31%)
  waiting for transfers between devices  16 us (25%)
  Pallas kernels  13.8 us (21%)
  blocking collectives  13.1 us (20%)
  local copies, waits for them, and re-layouts  0.88 us (1%)
  between operations  0.85 us (1%)
    ppermute x12, waiting for transfers between devices, to(): return lax.ppermute(value, 'row', [(i, target(i)) for i in range(rows)])  16 us
    all_to_all x1, blocking collectives, per_device(): pieces = lax.all_to_all(features, 'row', 0, 0, tiled=True)  13.1 us
    ppermute x12, starting transfers between devices, to(): return lax.ppermute(value, 'row', [(i, target(i)) for i in range(rows)])  12.9 us
    pallas_call x3, Pallas kernels, chunk_products(): pl.pallas_call(functools.partial(next_kernel, step, slots), out_shape=(ha...  7.82 us
    ppermute x1, starting transfers between devices, per_device(): inverse_panel = lax.ppermute(share, ('row', 'col'), swap)  6.97 us
    pallas_call x1, Pallas kernels, chunk_products(): pl.pallas_call(first_kernel, out_shape=(half, half, columns, columns, col...  5.17 us
  transfers between devices with their start and end apart: 13, of which 4 were waited for; matrix products, arithmetic and copies ran while one was open for 1% of the time, Pallas kernels for 9%

profile of v2, /device:TPU:1, one launch (start us, length us, event | category | flops | bytes accessed | tf_op | source)
XLA Modules:
  0.0 64.9 jit_solution(14897288903027640638)
XLA Ops:
  0.6 5.2 %product_0.1 = (f32[2,96,512]{2,1,0:T(8,128)S(1)}, f32[2,96,512]{2,1,0:T(8,128)S(1)}, f32[1536,384]{1,0:T(8,128)S(1)}, f32[1536,384]{1,0:T(8,128)S(1)}, f32[1536...) custom-call(s32[16,12]{1,0:T(8,128)} %blocks_hbm.1, s32[16]{0:T(128)} %counts.5, ...), custom_call_target="tpu_custom_call" | custom-call | tf_op jit(solution)/shard_map/product_0/pallas_call | solution.py:134
  5.8 2.6 %shard_map.59 = (f32[2,96,512]{2,1,0:T(8,128)S(1)}, f32[2,96,512]{2,1,0:T(8,128)S(1)}) custom-call(s32[16]{0:T(128)S(1)} %copy-done, f32[1536,384]{1,0:T(8,128)S(1)} %get-tuple-element.15.a_now, bf16[1536,512]{1,0:T(8,128)(2,1)S(1)} %get-tuple-element.16.f_high, bf16[1536,512]{1,0:T(8,128)(2,1)S(1)} %get-tuple-element.17.f_low), custom_call_target="tpu_custom_call" | custom-call | tf_op jit(solution)/shard_map/pallas_call | solution.py:154
  8.4 3.3 %collective-permute-start = (f32[2,96,512]{2,1,0:T(8,128)S(1)}, f32[2,96,512]{2,1,0:T(8,128)S(1)}, u32[]{:S(2)}, u32[]{:S(2)}) collective-permute-start(f32[2,96,512]{2,1,0:T(8,128)S(1)} %get-tuple-element.19), channel_id=1, source_target_pairs={{0,16},{16,0},{32,48},{48,32},{64,80},{80,64},{96,112},{112,96},{1... | collective-permute-start | bytes 1179656 | tf_op jit(solution)/shard_map/ppermute | solution.py:171
  11.7 0.1 collective-permute-start.4
  11.8 2.6 %shard_map.60 = (f32[2,96,512]{2,1,0:T(8,128)S(1)}, f32[2,96,512]{2,1,0:T(8,128)S(1)}) custom-call(s32[16]{0:T(128)S(1)} %copy-done, f32[1536,384]{1,0:T(8,128)S(1)} %get-tuple-element.20.a_now, bf16[1536,512]{1,0:T(8,128)(2,1)S(1)} %get-tuple-element.16.f_high, bf16[1536,512]{1,0:T(8,128)(2,1)S(1)} %get-tuple-element.17.f_low), custom_call_target="tpu_custom_call" | custom-call | tf_op jit(solution)/shard_map/pallas_call | solution.py:154
  14.4 0.5 collective-permute-start.2
  14.9 2.6 %shard_map.61 = (f32[2,96,512]{2,1,0:T(8,128)S(1)}, f32[2,96,512]{2,1,0:T(8,128)S(1)}) custom-call(s32[16]{0:T(128)S(1)} %copy-done, f32[1536,384]{1,0:T(8,128)S(1)} %get-tuple-element.25.a_now, bf16[1536,512]{1,0:T(8,128)(2,1)S(1)} %get-tuple-element.16.f_high, bf16[1536,512]{1,0:T(8,128)(2,1)S(1)} %get-tuple-element.17.f_low), custom_call_target="tpu_custom_call" | custom-call | tf_op jit(solution)/shard_map/pallas_call | solution.py:154
  17.6 0.2 collective-permute-start.8
  17.7 0.0 collective-permute-done
  17.8 0.1 add.36
  17.8 0.1 collective-permute-start.1
  17.9 0.0 collective-permute-done.4
  17.9 0.1 add.40
  18.0 1.5 %collective-permute-start.5 = (f32[96,512]{1,0:T(8,128)S(1)}, f32[96,512]{1,0:T(8,128)S(1)}, u32[]{:S(2)}, u32[]{:S(2)}) collective-permute-start(f32[96,512]{1,0:T(8,128)S(1)} %slice_bitcast_fusion.2), channel_id=1, source_target_pairs={{0,32},{16,48},{32,0},{48,16},{64,96},{80,112},{96,64},{112,80},{1... | collective-permute-start | bytes 589832 | tf_op jit(solution)/shard_map/ppermute | solution.py:171
  19.6 0.1 add.38
  19.6 0.1 collective-permute-start.3
  19.8 0.1 add.44
  19.8 1.5 %collective-permute-start.9 = (f32[96,512]{1,0:T(8,128)S(1)}, f32[96,512]{1,0:T(8,128)S(1)}, u32[]{:S(2)}, u32[]{:S(2)}) collective-permute-start(f32[96,512]{1,0:T(8,128)S(1)} %slice_bitcast_fusion), channel_id=1, source_target_pairs={{0,32},{16,48},{32,0},{48,16},{64,96},{80,112},{96,64},{112,80},{1... | collective-permute-start | bytes 589832 | tf_op jit(solution)/shard_map/ppermute | solution.py:171
  21.4 6.8 %collective-permute-done.5 = f32[96,512]{1,0:T(8,128)S(1)} collective-permute-done((f32[96,512]{1,0:T(8,128)S(1)}, f32[96,512]{1,0:T(8,128)S(1)}, u32[]{:S(2)}, u32[]{:S(2)}) %collective-permute-start.5) | collective-permute-done | bytes 196640 | tf_op jit(solution)/shard_map/ppermute | solution.py:171
  28.2 0.1 collective-permute-start.6
  28.3 2.7 %collective-permute-start.10 = (f32[96,256]{1,0:T(8,128)S(1)}, f32[96,256]{1,0:T(8,128)S(1)}, u32[]{:S(2)}, u32[]{:S(2)}) collective-permute-start(f32[96,256]{1,0:T(8,128)S(1)} %get-tuple-element.31), channel_id=1, source_target_pairs={{0,192},{16,208},{32,224},{48,240},{64,0},{80,16},{96,32},{112,48}... | collective-permute-start | bytes 294920 | tf_op jit(solution)/shard_map/ppermute | solution.py:171
  31.0 1.4 %collective-permute-done.3 = f32[96,512]{1,0:T(8,128)S(1)} collective-permute-done((f32[96,512]{1,0:T(8,128)S(1)}, f32[96,512]{1,0:T(8,128)S(1)}, u32[]{:S(2)}, u32[]{:S(2)}) %collective-permute-start.3) | collective-permute-done | bytes 196640 | tf_op jit(solution)/shard_map/ppermute | solution.py:171
  32.4 4.2 %collective-permute-done.9 = f32[96,512]{1,0:T(8,128)S(1)} collective-permute-done((f32[96,512]{1,0:T(8,128)S(1)}, f32[96,512]{1,0:T(8,128)S(1)}, u32[]{:S(2)}, u32[]{:S(2)}) %collective-permute-start.9) | collective-permute-done | bytes 196640 | tf_op jit(solution)/shard_map/ppermute | solution.py:171
  36.7 0.1 collective-permute-start.7
  36.9 2.7 %collective-permute-start.11 = (f32[96,512]{1,0:T(8,128)S(1)}, f32[96,512]{1,0:T(8,128)S(1)}, u32[]{:S(2)}, u32[]{:S(2)}) collective-permute-start(f32[96,512]{1,0:T(8,128)S(1)} %pad_maximum_fusion.1), channel_id=1, source_target_pairs={{0,192},{16,208},{32,224},{48,240},{64,0},{80,16},{96,32},{112,48}... | collective-permute-start | bytes 589832 | tf_op jit(solution)/shard_map/ppermute | solution.py:171
  39.6 3.6 %collective-permute-done.7 = f32[96,512]{1,0:T(8,128)S(1)} collective-permute-done((f32[96,512]{1,0:T(8,128)S(1)}, f32[96,512]{1,0:T(8,128)S(1)}, u32[]{:S(2)}, u32[]{:S(2)}) %collective-permute-start.7) | collective-permute-done | bytes 196640 | tf_op jit(solution)/shard_map/ppermute | solution.py:171
  43.2 0.1 fusion.5
  43.2 7.0 %collective-permute-start.12 = (f32[96,512]{1,0:T(8,128)S(1)}, f32[96,512]{1,0:T(8,128)S(1)}, u32[]{:S(2)}, u32[]{:S(2)}) collective-permute-start(f32[96,512]{1,0:T(8,128)S(1)} %fusion.5), channel_id=1, source_target_pairs={{0,8},{1,24},{2,40},{3,56},{4,64},{5,80},{6,96},{7,112},{8,136},{9... | collective-permute-start | bytes 589832 | tf_op jit(solution)/shard_map/ppermute | solution.py:192
  50.2 0.1 copy.6
  50.3 13.1 %all_to_all.5.pieces = f32[16,32,96]{2,1,0:T(8,128)S(1)} all-to-all(f32[16,32,96]{2,1,0:T(8,128)S(1)} %bitcast.30), channel_id=1, replica_groups=mesh['row'=16,'col'=16] {'row'}, dimensions={0} | all-to-all | bytes 393216 | tf_op jit(solution)/shard_map/all_to_all | solution.py:194
  63.5 0.8 %in_order.1 = f32[32,1536]{1,0:T(8,128)} custom-call(f32[16,32,96]{2,1,0:T(8,128)S(1)} %all_to_all.5.pieces), custom_call_target="tpu_custom_call" | custom-call | tf_op jit(solution)/shard_map/in_order/pallas_call | solution.py:210
  64.3 0.7 %copy.8 = f32[96,512]{1,0:T(8,128)} copy(f32[96,512]{1,0:T(8,128)S(1)} %collective-permute-done.12) | data formatting | bytes 393216
  (21 shorter events, 0.3 us)
Async XLA Ops:
  0.6 5.2 %copy-start = (s32[16]{0:T(128)S(1)}, s32[16]{0:T(128)}, u32[]{:S(2)}) copy-start(s32[16]{0:T(128)} %counts.5) | copy-start | bytes 196
  8.4 9.3 %collective-permute-start = (f32[2,96,512]{2,1,0:T(8,128)S(1)}, f32[2,96,512]{2,1,0:T(8,128)S(1)}, u32[]{:S(2)}, u32[]{:S(2)}) collective-permute-start(f32[2,96,512]{2,1,0:T(8,128)S(1)} %get-tuple-element.19), channel_id=1, source_target_pairs={{0,16},{16,0},{32,48},{48,32},{64,80},{80,64},{96,112},{112,96},{1... | collective-permute-start | bytes 1179656 | tf_op jit(solution)/shard_map/ppermute | solution.py:171
  11.7 6.2 %collective-permute-start.4 = (f32[2,96,512]{2,1,0:T(8,128)S(1)}, f32[2,96,512]{2,1,0:T(8,128)S(1)}, u32[]{:S(2)}, u32[]{:S(2)}) collective-permute-start(f32[2,96,512]{2,1,0:T(8,128)S(1)} %get-tuple-element.24), channel_id=1, source_target_pairs={{0,16},{16,0},{32,48},{48,32},{64,80},{80,64},{96,112},{112,96},{1... | collective-permute-start | bytes 1179656 | tf_op jit(solution)/shard_map/ppermute | solution.py:171
  14.4 5.1 %collective-permute-start.2 = (f32[2,96,512]{2,1,0:T(8,128)S(1)}, f32[2,96,512]{2,1,0:T(8,128)S(1)}, u32[]{:S(2)}, u32[]{:S(2)}) collective-permute-start(f32[2,96,512]{2,1,0:T(8,128)S(1)} %get-tuple-element.22), channel_id=1, source_target_pairs={{0,16},{16,0},{32,48},{48,32},{64,80},{80,64},{96,112},{112,96},{1... | collective-permute-start | bytes 1179656 | tf_op jit(solution)/shard_map/ppermute | solution.py:171
  17.6 2.2 %collective-permute-start.8 = (f32[2,96,512]{2,1,0:T(8,128)S(1)}, f32[2,96,512]{2,1,0:T(8,128)S(1)}, u32[]{:S(2)}, u32[]{:S(2)}) collective-permute-start(f32[2,96,512]{2,1,0:T(8,128)S(1)} %get-tuple-element.27), channel_id=1, source_target_pairs={{0,16},{16,0},{32,48},{48,32},{64,80},{80,64},{96,112},{112,96},{1... | collective-permute-start | bytes 1179656 | tf_op jit(solution)/shard_map/ppermute | solution.py:171
  17.8 21.8 %collective-permute-start.1 = (f32[96,512]{1,0:T(8,128)S(1)}, f32[96,512]{1,0:T(8,128)S(1)}, u32[]{:S(2)}, u32[]{:S(2)}) collective-permute-start(f32[96,512]{1,0:T(8,128)S(1)} %slice_bitcast_fusion.6), channel_id=1, source_target_pairs={{0,32},{16,48},{32,0},{48,16},{64,96},{80,112},{96,64},{112,80},{1... | collective-permute-start | bytes 589832 | tf_op jit(solution)/shard_map/ppermute | solution.py:171
  18.0 10.2 %collective-permute-start.5 = (f32[96,512]{1,0:T(8,128)S(1)}, f32[96,512]{1,0:T(8,128)S(1)}, u32[]{:S(2)}, u32[]{:S(2)}) collective-permute-start(f32[96,512]{1,0:T(8,128)S(1)} %slice_bitcast_fusion.2), channel_id=1, source_target_pairs={{0,32},{16,48},{32,0},{48,16},{64,96},{80,112},{96,64},{112,80},{1... | collective-permute-start | bytes 589832 | tf_op jit(solution)/shard_map/ppermute | solution.py:171
  19.6 12.8 %collective-permute-start.3 = (f32[96,512]{1,0:T(8,128)S(1)}, f32[96,512]{1,0:T(8,128)S(1)}, u32[]{:S(2)}, u32[]{:S(2)}) collective-permute-start(f32[96,512]{1,0:T(8,128)S(1)} %slice_bitcast_fusion.4), channel_id=1, source_target_pairs={{0,32},{16,48},{32,0},{48,16},{64,96},{80,112},{96,64},{112,80},{1... | collective-permute-start | bytes 589832 | tf_op jit(solution)/shard_map/ppermute | solution.py:171
  19.8 16.8 %collective-permute-start.9 = (f32[96,512]{1,0:T(8,128)S(1)}, f32[96,512]{1,0:T(8,128)S(1)}, u32[]{:S(2)}, u32[]{:S(2)}) collective-permute-start(f32[96,512]{1,0:T(8,128)S(1)} %slice_bitcast_fusion), channel_id=1, source_target_pairs={{0,32},{16,48},{32,0},{48,16},{64,96},{80,112},{96,64},{112,80},{1... | collective-permute-start | bytes 589832 | tf_op jit(solution)/shard_map/ppermute | solution.py:171
  28.2 8.4 %collective-permute-start.6 = (f32[96,256]{1,0:T(8,128)S(1)}, f32[96,256]{1,0:T(8,128)S(1)}, u32[]{:S(2)}, u32[]{:S(2)}) collective-permute-start(f32[96,256]{1,0:T(8,128)S(1)} %get-tuple-element.30), channel_id=1, source_target_pairs={{0,64},{16,80},{32,96},{48,112},{64,128},{80,144},{96,160},{112,17... | collective-permute-start | bytes 294920 | tf_op jit(solution)/shard_map/ppermute | solution.py:171
  28.3 8.5 %collective-permute-start.10 = (f32[96,256]{1,0:T(8,128)S(1)}, f32[96,256]{1,0:T(8,128)S(1)}, u32[]{:S(2)}, u32[]{:S(2)}) collective-permute-start(f32[96,256]{1,0:T(8,128)S(1)} %get-tuple-element.31), channel_id=1, source_target_pairs={{0,192},{16,208},{32,224},{48,240},{64,0},{80,16},{96,32},{112,48}... | collective-permute-start | bytes 294920 | tf_op jit(solution)/shard_map/ppermute | solution.py:171
  36.7 6.5 %collective-permute-start.7 = (f32[96,512]{1,0:T(8,128)S(1)}, f32[96,512]{1,0:T(8,128)S(1)}, u32[]{:S(2)}, u32[]{:S(2)}) collective-permute-start(f32[96,512]{1,0:T(8,128)S(1)} %pad_maximum_fusion), channel_id=1, source_target_pairs={{0,64},{16,80},{32,96},{48,112},{64,128},{80,144},{96,160},{112,17... | collective-permute-start | bytes 589832 | tf_op jit(solution)/shard_map/ppermute | solution.py:171
  36.9 6.3 %collective-permute-start.11 = (f32[96,512]{1,0:T(8,128)S(1)}, f32[96,512]{1,0:T(8,128)S(1)}, u32[]{:S(2)}, u32[]{:S(2)}) collective-permute-start(f32[96,512]{1,0:T(8,128)S(1)} %pad_maximum_fusion.1), channel_id=1, source_target_pairs={{0,192},{16,208},{32,224},{48,240},{64,0},{80,16},{96,32},{112,48}... | collective-permute-start | bytes 589832 | tf_op jit(solution)/shard_map/ppermute | solution.py:171
  43.2 21.0 %collective-permute-start.12 = (f32[96,512]{1,0:T(8,128)S(1)}, f32[96,512]{1,0:T(8,128)S(1)}, u32[]{:S(2)}, u32[]{:S(2)}) collective-permute-start(f32[96,512]{1,0:T(8,128)S(1)} %fusion.5), channel_id=1, source_target_pairs={{0,8},{1,24},{2,40},{3,56},{4,64},{5,80},{6,96},{7,112},{8,136},{9... | collective-permute-start | bytes 589832 | tf_op jit(solution)/shard_map/ppermute | solution.py:192

commit v3 on v2

--- a/solution.py
+++ b/solution.py
@@ -192,10 +192,11 @@
     inverse_panel = lax.ppermute(share, ("row", "col"), swap)
     features = share.T.reshape(rows, width // rows, share_rows)
     pieces = lax.all_to_all(features, "row", 0, 0, tiled=True)
-    return inverse_panel, in_order(pieces)
-
-
-def in_order_kernel(pieces, out):
+    return in_order(inverse_panel, pieces)
+
+
+def in_order_kernel(panel, pieces, panel_out, out):
+    panel_out[...] = panel[...]
     rows = pieces.shape[0]
     c = lax.axis_index("col")
     parts = []
@@ -205,16 +206,19 @@
     out[...] = jnp.concatenate(parts, axis=1)
 
 
-def in_order(pieces):
+def in_order(panel, pieces):
     count, height, columns = pieces.shape
     return pl.pallas_call(
         in_order_kernel,
-        out_shape=jax.ShapeDtypeStruct((height, count * columns), pieces.dtype),
-        in_specs=[VMEM],
-        out_specs=VMEM,
+        out_shape=(
+            jax.ShapeDtypeStruct(panel.shape, panel.dtype),
+            jax.ShapeDtypeStruct((height, count * columns), pieces.dtype),
+        ),
+        in_specs=[VMEM, VMEM],
+        out_specs=(VMEM, VMEM),
         compiler_params=pltpu.CompilerParams(vmem_limit_bytes=8 * 1024 * 1024),
         name="in_order",
-    )(pieces)
+    )(panel, pieces)
 
 
 def solution(mesh):

time: 65.1 us -> 64.4 us (0.989)
  local copies, waits for them, and re-layouts: 0.88 us -> 0.2 us
    unnamed x3 -> x2, local copies, waits for them, and re-layouts: 0.68 us -> 0.01 us
  transfers between devices with their start and end apart: 13 -> 13, of which waited for: 4 -> 4; matrix products, arithmetic and copies ran while one was open for 1% -> 1% of each run, Pallas kernels for 9% -> 8%
where the time goes in v3:
time: 64.4 us; the launch traced here: 64.3 us
  starting transfers between devices  19.8 us (31%)
  waiting for transfers between devices  16 us (25%)
  Pallas kernels  13.8 us (21%)
  blocking collectives  13.1 us (20%)
  between operations  0.85 us (1%)
    ppermute x12, waiting for transfers between devices, to(): return lax.ppermute(value, 'row', [(i, target(i)) for i in range(rows)])  16 us
    all_to_all x1, blocking collectives, per_device(): pieces = lax.all_to_all(features, 'row', 0, 0, tiled=True)  13.1 us
    ppermute x12, starting transfers between devices, to(): return lax.ppermute(value, 'row', [(i, target(i)) for i in range(rows)])  12.9 us
    pallas_call x3, Pallas kernels, chunk_products(): pl.pallas_call(functools.partial(next_kernel, step, slots), out_shape=(ha...  7.82 us
    ppermute x1, starting transfers between devices, per_device(): inverse_panel = lax.ppermute(share, ('row', 'col'), swap)  6.96 us
    pallas_call x1, Pallas kernels, chunk_products(): pl.pallas_call(first_kernel, out_shape=(half, half, columns, columns, col...  5.17 us
  transfers between devices with their start and end apart: 13, of which 4 were waited for; matrix products, arithmetic and copies ran while one was open for 1% of the time, Pallas kernels for 8%

profile of v3, /device:TPU:1, one launch (start us, length us, event | category | flops | bytes accessed | tf_op | source)
XLA Modules:
  0.0 64.3 jit_solution(1216118134595687533)
XLA Ops:
  0.6 5.2 %product_0.1 = (f32[2,96,512]{2,1,0:T(8,128)S(1)}, f32[2,96,512]{2,1,0:T(8,128)S(1)}, f32[1536,384]{1,0:T(8,128)S(1)}, f32[1536,384]{1,0:T(8,128)S(1)}, f32[1536...) custom-call(s32[16,12]{1,0:T(8,128)} %blocks_hbm.1, s32[16]{0:T(128)} %counts.5, ...), custom_call_target="tpu_custom_call" | custom-call | tf_op jit(solution)/shard_map/product_0/pallas_call | solution.py:134
  5.8 2.6 %shard_map.59 = (f32[2,96,512]{2,1,0:T(8,128)S(1)}, f32[2,96,512]{2,1,0:T(8,128)S(1)}) custom-call(s32[16]{0:T(128)S(1)} %copy-done, f32[1536,384]{1,0:T(8,128)S(1)} %get-tuple-element.15.a_now, bf16[1536,512]{1,0:T(8,128)(2,1)S(1)} %get-tuple-element.16.f_high, bf16[1536,512]{1,0:T(8,128)(2,1)S(1)} %get-tuple-element.17.f_low), custom_call_target="tpu_custom_call" | custom-call | tf_op jit(solution)/shard_map/pallas_call | solution.py:154
  8.4 3.3 %collective-permute-start = (f32[2,96,512]{2,1,0:T(8,128)S(1)}, f32[2,96,512]{2,1,0:T(8,128)S(1)}, u32[]{:S(2)}, u32[]{:S(2)}) collective-permute-start(f32[2,96,512]{2,1,0:T(8,128)S(1)} %get-tuple-element.19), channel_id=1, source_target_pairs={{0,16},{16,0},{32,48},{48,32},{64,80},{80,64},{96,112},{112,96},{1... | collective-permute-start | bytes 1179656 | tf_op jit(solution)/shard_map/ppermute | solution.py:171
  11.7 0.1 collective-permute-start.4
  11.8 2.6 %shard_map.60 = (f32[2,96,512]{2,1,0:T(8,128)S(1)}, f32[2,96,512]{2,1,0:T(8,128)S(1)}) custom-call(s32[16]{0:T(128)S(1)} %copy-done, f32[1536,384]{1,0:T(8,128)S(1)} %get-tuple-element.20.a_now, bf16[1536,512]{1,0:T(8,128)(2,1)S(1)} %get-tuple-element.16.f_high, bf16[1536,512]{1,0:T(8,128)(2,1)S(1)} %get-tuple-element.17.f_low), custom_call_target="tpu_custom_call" | custom-call | tf_op jit(solution)/shard_map/pallas_call | solution.py:154
  14.5 0.5 collective-permute-start.2
  14.9 2.6 %shard_map.61 = (f32[2,96,512]{2,1,0:T(8,128)S(1)}, f32[2,96,512]{2,1,0:T(8,128)S(1)}) custom-call(s32[16]{0:T(128)S(1)} %copy-done, f32[1536,384]{1,0:T(8,128)S(1)} %get-tuple-element.25.a_now, bf16[1536,512]{1,0:T(8,128)(2,1)S(1)} %get-tuple-element.16.f_high, bf16[1536,512]{1,0:T(8,128)(2,1)S(1)} %get-tuple-element.17.f_low), custom_call_target="tpu_custom_call" | custom-call | tf_op jit(solution)/shard_map/pallas_call | solution.py:154
  17.6 0.2 collective-permute-start.8
  17.8 0.1 add.36
  17.8 0.1 collective-permute-start.1
  17.9 0.0 collective-permute-done.4
  17.9 0.1 add.40
  18.0 1.5 %collective-permute-start.5 = (f32[96,512]{1,0:T(8,128)S(1)}, f32[96,512]{1,0:T(8,128)S(1)}, u32[]{:S(2)}, u32[]{:S(2)}) collective-permute-start(f32[96,512]{1,0:T(8,128)S(1)} %slice_bitcast_fusion.2), channel_id=1, source_target_pairs={{0,32},{16,48},{32,0},{48,16},{64,96},{80,112},{96,64},{112,80},{1... | collective-permute-start | bytes 589832 | tf_op jit(solution)/shard_map/ppermute | solution.py:171
  19.6 0.0 collective-permute-done.2
  19.6 0.1 add.38
  19.6 0.1 collective-permute-start.3
  19.8 0.0 collective-permute-done.8
  19.8 0.1 add.44
  19.8 1.5 %collective-permute-start.9 = (f32[96,512]{1,0:T(8,128)S(1)}, f32[96,512]{1,0:T(8,128)S(1)}, u32[]{:S(2)}, u32[]{:S(2)}) collective-permute-start(f32[96,512]{1,0:T(8,128)S(1)} %slice_bitcast_fusion), channel_id=1, source_target_pairs={{0,32},{16,48},{32,0},{48,16},{64,96},{80,112},{96,64},{112,80},{1... | collective-permute-start | bytes 589832 | tf_op jit(solution)/shard_map/ppermute | solution.py:171
  21.4 6.8 %collective-permute-done.5 = f32[96,512]{1,0:T(8,128)S(1)} collective-permute-done((f32[96,512]{1,0:T(8,128)S(1)}, f32[96,512]{1,0:T(8,128)S(1)}, u32[]{:S(2)}, u32[]{:S(2)}) %collective-permute-start.5) | collective-permute-done | bytes 196640 | tf_op jit(solution)/shard_map/ppermute | solution.py:171
  28.2 0.1 collective-permute-start.6
  28.3 2.7 %collective-permute-start.10 = (f32[96,256]{1,0:T(8,128)S(1)}, f32[96,256]{1,0:T(8,128)S(1)}, u32[]{:S(2)}, u32[]{:S(2)}) collective-permute-start(f32[96,256]{1,0:T(8,128)S(1)} %get-tuple-element.31), channel_id=1, source_target_pairs={{0,192},{16,208},{32,224},{48,240},{64,0},{80,16},{96,32},{112,48}... | collective-permute-start | bytes 294920 | tf_op jit(solution)/shard_map/ppermute | solution.py:171
  31.0 1.4 %collective-permute-done.3 = f32[96,512]{1,0:T(8,128)S(1)} collective-permute-done((f32[96,512]{1,0:T(8,128)S(1)}, f32[96,512]{1,0:T(8,128)S(1)}, u32[]{:S(2)}, u32[]{:S(2)}) %collective-permute-start.3) | collective-permute-done | bytes 196640 | tf_op jit(solution)/shard_map/ppermute | solution.py:171
  32.4 4.2 %collective-permute-done.9 = f32[96,512]{1,0:T(8,128)S(1)} collective-permute-done((f32[96,512]{1,0:T(8,128)S(1)}, f32[96,512]{1,0:T(8,128)S(1)}, u32[]{:S(2)}, u32[]{:S(2)}) %collective-permute-start.9) | collective-permute-done | bytes 196640 | tf_op jit(solution)/shard_map/ppermute | solution.py:171
  36.7 0.1 collective-permute-start.7
  36.9 2.7 %collective-permute-start.11 = (f32[96,512]{1,0:T(8,128)S(1)}, f32[96,512]{1,0:T(8,128)S(1)}, u32[]{:S(2)}, u32[]{:S(2)}) collective-permute-start(f32[96,512]{1,0:T(8,128)S(1)} %pad_maximum_fusion.1), channel_id=1, source_target_pairs={{0,192},{16,208},{32,224},{48,240},{64,0},{80,16},{96,32},{112,48}... | collective-permute-start | bytes 589832 | tf_op jit(solution)/shard_map/ppermute | solution.py:171
  39.6 3.6 %collective-permute-done.7 = f32[96,512]{1,0:T(8,128)S(1)} collective-permute-done((f32[96,512]{1,0:T(8,128)S(1)}, f32[96,512]{1,0:T(8,128)S(1)}, u32[]{:S(2)}, u32[]{:S(2)}) %collective-permute-start.7) | collective-permute-done | bytes 196640 | tf_op jit(solution)/shard_map/ppermute | solution.py:171
  43.2 0.1 fusion.5
  43.3 7.0 %collective-permute-start.12 = (f32[96,512]{1,0:T(8,128)S(1)}, f32[96,512]{1,0:T(8,128)S(1)}, u32[]{:S(2)}, u32[]{:S(2)}) collective-permute-start(f32[96,512]{1,0:T(8,128)S(1)} %fusion.5), channel_id=1, source_target_pairs={{0,8},{1,24},{2,40},{3,56},{4,64},{5,80},{6,96},{7,112},{8,136},{9... | collective-permute-start | bytes 589832 | tf_op jit(solution)/shard_map/ppermute | solution.py:192
  50.2 0.1 copy.6
  50.3 13.1 %all_to_all.5.pieces = f32[16,32,96]{2,1,0:T(8,128)S(1)} all-to-all(f32[16,32,96]{2,1,0:T(8,128)S(1)} %bitcast.30), channel_id=1, replica_groups=mesh['row'=16,'col'=16] {'row'}, dimensions={0} | all-to-all | bytes 393216 | tf_op jit(solution)/shard_map/all_to_all | solution.py:194
  63.5 0.8 %in_order.1 = (f32[96,512]{1,0:T(8,128)}, f32[32,1536]{1,0:T(8,128)}) custom-call(f32[96,512]{1,0:T(8,128)S(1)} %collective-permute-done.12.panel, f32[16,32,96]{2,1,0:T(8,128)S(1)} %all_to_all.5.pieces), custom_call_target="tpu_custom_call" | custom-call | tf_op jit(solution)/shard_map/in_order/pallas_call | solution.py:211
  (20 shorter events, 0.3 us)
Async XLA Ops:
  0.6 5.2 %copy-start = (s32[16]{0:T(128)S(1)}, s32[16]{0:T(128)}, u32[]{:S(2)}) copy-start(s32[16]{0:T(128)} %counts.5) | copy-start | bytes 196
  8.4 9.3 %collective-permute-start = (f32[2,96,512]{2,1,0:T(8,128)S(1)}, f32[2,96,512]{2,1,0:T(8,128)S(1)}, u32[]{:S(2)}, u32[]{:S(2)}) collective-permute-start(f32[2,96,512]{2,1,0:T(8,128)S(1)} %get-tuple-element.19), channel_id=1, source_target_pairs={{0,16},{16,0},{32,48},{48,32},{64,80},{80,64},{96,112},{112,96},{1... | collective-permute-start | bytes 1179656 | tf_op jit(solution)/shard_map/ppermute | solution.py:171
  11.7 6.2 %collective-permute-start.4 = (f32[2,96,512]{2,1,0:T(8,128)S(1)}, f32[2,96,512]{2,1,0:T(8,128)S(1)}, u32[]{:S(2)}, u32[]{:S(2)}) collective-permute-start(f32[2,96,512]{2,1,0:T(8,128)S(1)} %get-tuple-element.24), channel_id=1, source_target_pairs={{0,16},{16,0},{32,48},{48,32},{64,80},{80,64},{96,112},{112,96},{1... | collective-permute-start | bytes 1179656 | tf_op jit(solution)/shard_map/ppermute | solution.py:171
  14.5 5.1 %collective-permute-start.2 = (f32[2,96,512]{2,1,0:T(8,128)S(1)}, f32[2,96,512]{2,1,0:T(8,128)S(1)}, u32[]{:S(2)}, u32[]{:S(2)}) collective-permute-start(f32[2,96,512]{2,1,0:T(8,128)S(1)} %get-tuple-element.22), channel_id=1, source_target_pairs={{0,16},{16,0},{32,48},{48,32},{64,80},{80,64},{96,112},{112,96},{1... | collective-permute-start | bytes 1179656 | tf_op jit(solution)/shard_map/ppermute | solution.py:171
  17.6 2.2 %collective-permute-start.8 = (f32[2,96,512]{2,1,0:T(8,128)S(1)}, f32[2,96,512]{2,1,0:T(8,128)S(1)}, u32[]{:S(2)}, u32[]{:S(2)}) collective-permute-start(f32[2,96,512]{2,1,0:T(8,128)S(1)} %get-tuple-element.27), channel_id=1, source_target_pairs={{0,16},{16,0},{32,48},{48,32},{64,80},{80,64},{96,112},{112,96},{1... | collective-permute-start | bytes 1179656 | tf_op jit(solution)/shard_map/ppermute | solution.py:171
  17.8 21.8 %collective-permute-start.1 = (f32[96,512]{1,0:T(8,128)S(1)}, f32[96,512]{1,0:T(8,128)S(1)}, u32[]{:S(2)}, u32[]{:S(2)}) collective-permute-start(f32[96,512]{1,0:T(8,128)S(1)} %slice_bitcast_fusion.6), channel_id=1, source_target_pairs={{0,32},{16,48},{32,0},{48,16},{64,96},{80,112},{96,64},{112,80},{1... | collective-permute-start | bytes 589832 | tf_op jit(solution)/shard_map/ppermute | solution.py:171
  18.0 10.2 %collective-permute-start.5 = (f32[96,512]{1,0:T(8,128)S(1)}, f32[96,512]{1,0:T(8,128)S(1)}, u32[]{:S(2)}, u32[]{:S(2)}) collective-permute-start(f32[96,512]{1,0:T(8,128)S(1)} %slice_bitcast_fusion.2), channel_id=1, source_target_pairs={{0,32},{16,48},{32,0},{48,16},{64,96},{80,112},{96,64},{112,80},{1... | collective-permute-start | bytes 589832 | tf_op jit(solution)/shard_map/ppermute | solution.py:171
  19.6 12.8 %collective-permute-start.3 = (f32[96,512]{1,0:T(8,128)S(1)}, f32[96,512]{1,0:T(8,128)S(1)}, u32[]{:S(2)}, u32[]{:S(2)}) collective-permute-start(f32[96,512]{1,0:T(8,128)S(1)} %slice_bitcast_fusion.4), channel_id=1, source_target_pairs={{0,32},{16,48},{32,0},{48,16},{64,96},{80,112},{96,64},{112,80},{1... | collective-permute-start | bytes 589832 | tf_op jit(solution)/shard_map/ppermute | solution.py:171
  19.8 16.8 %collective-permute-start.9 = (f32[96,512]{1,0:T(8,128)S(1)}, f32[96,512]{1,0:T(8,128)S(1)}, u32[]{:S(2)}, u32[]{:S(2)}) collective-permute-start(f32[96,512]{1,0:T(8,128)S(1)} %slice_bitcast_fusion), channel_id=1, source_target_pairs={{0,32},{16,48},{32,0},{48,16},{64,96},{80,112},{96,64},{112,80},{1... | collective-permute-start | bytes 589832 | tf_op jit(solution)/shard_map/ppermute | solution.py:171
  28.2 8.4 %collective-permute-start.6 = (f32[96,256]{1,0:T(8,128)S(1)}, f32[96,256]{1,0:T(8,128)S(1)}, u32[]{:S(2)}, u32[]{:S(2)}) collective-permute-start(f32[96,256]{1,0:T(8,128)S(1)} %get-tuple-element.30), channel_id=1, source_target_pairs={{0,64},{16,80},{32,96},{48,112},{64,128},{80,144},{96,160},{112,17... | collective-permute-start | bytes 294920 | tf_op jit(solution)/shard_map/ppermute | solution.py:171
  28.3 8.5 %collective-permute-start.10 = (f32[96,256]{1,0:T(8,128)S(1)}, f32[96,256]{1,0:T(8,128)S(1)}, u32[]{:S(2)}, u32[]{:S(2)}) collective-permute-start(f32[96,256]{1,0:T(8,128)S(1)} %get-tuple-element.31), channel_id=1, source_target_pairs={{0,192},{16,208},{32,224},{48,240},{64,0},{80,16},{96,32},{112,48}... | collective-permute-start | bytes 294920 | tf_op jit(solution)/shard_map/ppermute | solution.py:171
  36.7 6.5 %collective-permute-start.7 = (f32[96,512]{1,0:T(8,128)S(1)}, f32[96,512]{1,0:T(8,128)S(1)}, u32[]{:S(2)}, u32[]{:S(2)}) collective-permute-start(f32[96,512]{1,0:T(8,128)S(1)} %pad_maximum_fusion), channel_id=1, source_target_pairs={{0,64},{16,80},{32,96},{48,112},{64,128},{80,144},{96,160},{112,17... | collective-permute-start | bytes 589832 | tf_op jit(solution)/shard_map/ppermute | solution.py:171
  36.9 6.3 %collective-permute-start.11 = (f32[96,512]{1,0:T(8,128)S(1)}, f32[96,512]{1,0:T(8,128)S(1)}, u32[]{:S(2)}, u32[]{:S(2)}) collective-permute-start(f32[96,512]{1,0:T(8,128)S(1)} %pad_maximum_fusion.1), channel_id=1, source_target_pairs={{0,192},{16,208},{32,224},{48,240},{64,0},{80,16},{96,32},{112,48}... | collective-permute-start | bytes 589832 | tf_op jit(solution)/shard_map/ppermute | solution.py:171
  43.3 20.2 %collective-permute-start.12 = (f32[96,512]{1,0:T(8,128)S(1)}, f32[96,512]{1,0:T(8,128)S(1)}, u32[]{:S(2)}, u32[]{:S(2)}) collective-permute-start(f32[96,512]{1,0:T(8,128)S(1)} %fusion.5), channel_id=1, source_target_pairs={{0,8},{1,24},{2,40},{3,56},{4,64},{5,80},{6,96},{7,112},{8,136},{9... | collective-permute-start | bytes 589832 | tf_op jit(solution)/shard_map/ppermute | solution.py:192

commit v4 on v3

--- a/solution.py
+++ b/solution.py
@@ -17,7 +17,7 @@
 
 
 def share_of(r, c):
-    return RING * chunk_of(r // RING, c) + 2 * (r % 2) + (r // 2) % 2
+    return RING * chunk_of(r // RING, c) + 2 * ((r + r // 2) % 2) + (r // 2) % 2
 
 
 def emit_chunk(blocks_count, chunk, a, f_high, f_low, acc, keep_ref, send_ref):
@@ -38,8 +38,8 @@
     core, y = r % 2, (r // 2) % 2
     for other in range(2):
         along_y = y if other == 0 else 1 - y
-        keep_ref[other] = acc[pl.ds((2 * core + along_y) * share, share), :]
-        send_ref[other] = acc[pl.ds((2 * (1 - core) + along_y) * share, share), :]
+        keep_ref[other] = acc[pl.ds((2 * ((core + along_y) % 2) + along_y) * share, share), :]
+        send_ref[other] = acc[pl.ds((2 * ((core + along_y + 1) % 2) + along_y) * share, share), :]
 
 
 def column_copies(ahead, blocks, a_hbm, target, sems):
@@ -202,7 +202,7 @@
     parts = []
     for s in range(rows):
         x = (2 * (c // RING) + 2 * RING + 2 - s // RING) % RING
-        parts.append(pieces[RING * x + 2 * (s % 2) + (s // 2) % 2])
+        parts.append(pieces[RING * x + 2 * (s % 2) + (s + s // 2) % 2])
     out[...] = jnp.concatenate(parts, axis=1)
 
 

time: 64.4 us -> 64.1 us (level)
  no operation moved by 1% of the time
where the time goes in v4:
time: 64.1 us; the launch traced here: 64 us
  starting transfers between devices  19.8 us (31%)
  waiting for transfers between devices  16 us (25%)
  Pallas kernels  13.8 us (22%)
  blocking collectives  12.8 us (20%)
  between operations  0.85 us (1%)
    ppermute x12, waiting for transfers between devices, to(): return lax.ppermute(value, 'row', [(i, target(i)) for i in range(rows)])  16 us
    ppermute x12, starting transfers between devices, to(): return lax.ppermute(value, 'row', [(i, target(i)) for i in range(rows)])  12.9 us
    all_to_all x1, blocking collectives, per_device(): pieces = lax.all_to_all(features, 'row', 0, 0, tiled=True)  12.8 us
    pallas_call x3, Pallas kernels, chunk_products(): pl.pallas_call(functools.partial(next_kernel, step, slots), out_shape=(ha...  7.82 us
    ppermute x1, starting transfers between devices, per_device(): inverse_panel = lax.ppermute(share, ('row', 'col'), swap)  6.96 us
    pallas_call x1, Pallas kernels, chunk_products(): pl.pallas_call(first_kernel, out_shape=(half, half, columns, columns, col...  5.17 us
  transfers between devices with their start and end apart: 13, of which 4 were waited for; matrix products, arithmetic and copies ran while one was open for 1% of the time, Pallas kernels for 8%

profile of v4, /device:TPU:1, one launch (start us, length us, event | category | flops | bytes accessed | tf_op | source)
XLA Modules:
  0.0 64.0 jit_solution(10093160806675778079)
XLA Ops:
  0.6 5.2 %product_0.1 = (f32[2,96,512]{2,1,0:T(8,128)S(1)}, f32[2,96,512]{2,1,0:T(8,128)S(1)}, f32[1536,384]{1,0:T(8,128)S(1)}, f32[1536,384]{1,0:T(8,128)S(1)}, f32[1536...) custom-call(s32[16,12]{1,0:T(8,128)} %blocks_hbm.1, s32[16]{0:T(128)} %counts.5, ...), custom_call_target="tpu_custom_call" | custom-call | tf_op jit(solution)/shard_map/product_0/pallas_call | solution.py:134
  5.8 2.6 %shard_map.59 = (f32[2,96,512]{2,1,0:T(8,128)S(1)}, f32[2,96,512]{2,1,0:T(8,128)S(1)}) custom-call(s32[16]{0:T(128)S(1)} %copy-done, f32[1536,384]{1,0:T(8,128)S(1)} %get-tuple-element.15.a_now, bf16[1536,512]{1,0:T(8,128)(2,1)S(1)} %get-tuple-element.16.f_high, bf16[1536,512]{1,0:T(8,128)(2,1)S(1)} %get-tuple-element.17.f_low), custom_call_target="tpu_custom_call" | custom-call | tf_op jit(solution)/shard_map/pallas_call | solution.py:154
  8.4 3.3 %collective-permute-start = (f32[2,96,512]{2,1,0:T(8,128)S(1)}, f32[2,96,512]{2,1,0:T(8,128)S(1)}, u32[]{:S(2)}, u32[]{:S(2)}) collective-permute-start(f32[2,96,512]{2,1,0:T(8,128)S(1)} %get-tuple-element.19), channel_id=1, source_target_pairs={{0,16},{16,0},{32,48},{48,32},{64,80},{80,64},{96,112},{112,96},{1... | collective-permute-start | bytes 1179656 | tf_op jit(solution)/shard_map/ppermute | solution.py:171
  11.7 0.1 collective-permute-start.4
  11.8 2.6 %shard_map.60 = (f32[2,96,512]{2,1,0:T(8,128)S(1)}, f32[2,96,512]{2,1,0:T(8,128)S(1)}) custom-call(s32[16]{0:T(128)S(1)} %copy-done, f32[1536,384]{1,0:T(8,128)S(1)} %get-tuple-element.20.a_now, bf16[1536,512]{1,0:T(8,128)(2,1)S(1)} %get-tuple-element.16.f_high, bf16[1536,512]{1,0:T(8,128)(2,1)S(1)} %get-tuple-element.17.f_low), custom_call_target="tpu_custom_call" | custom-call | tf_op jit(solution)/shard_map/pallas_call | solution.py:154
  14.5 0.5 collective-permute-start.2
  14.9 2.6 %shard_map.61 = (f32[2,96,512]{2,1,0:T(8,128)S(1)}, f32[2,96,512]{2,1,0:T(8,128)S(1)}) custom-call(s32[16]{0:T(128)S(1)} %copy-done, f32[1536,384]{1,0:T(8,128)S(1)} %get-tuple-element.25.a_now, bf16[1536,512]{1,0:T(8,128)(2,1)S(1)} %get-tuple-element.16.f_high, bf16[1536,512]{1,0:T(8,128)(2,1)S(1)} %get-tuple-element.17.f_low), custom_call_target="tpu_custom_call" | custom-call | tf_op jit(solution)/shard_map/pallas_call | solution.py:154
  17.6 0.2 collective-permute-start.8
  17.8 0.1 add.36
  17.8 0.1 collective-permute-start.1
  17.9 0.0 collective-permute-done.4
  17.9 0.1 add.40
  18.0 1.5 %collective-permute-start.5 = (f32[96,512]{1,0:T(8,128)S(1)}, f32[96,512]{1,0:T(8,128)S(1)}, u32[]{:S(2)}, u32[]{:S(2)}) collective-permute-start(f32[96,512]{1,0:T(8,128)S(1)} %slice_bitcast_fusion.2), channel_id=1, source_target_pairs={{0,32},{16,48},{32,0},{48,16},{64,96},{80,112},{96,64},{112,80},{1... | collective-permute-start | bytes 589832 | tf_op jit(solution)/shard_map/ppermute | solution.py:171
  19.6 0.0 collective-permute-done.2
  19.6 0.1 add.38
  19.6 0.1 collective-permute-start.3
  19.8 0.0 collective-permute-done.8
  19.8 0.1 add.44
  19.8 1.5 %collective-permute-start.9 = (f32[96,512]{1,0:T(8,128)S(1)}, f32[96,512]{1,0:T(8,128)S(1)}, u32[]{:S(2)}, u32[]{:S(2)}) collective-permute-start(f32[96,512]{1,0:T(8,128)S(1)} %slice_bitcast_fusion), channel_id=1, source_target_pairs={{0,32},{16,48},{32,0},{48,16},{64,96},{80,112},{96,64},{112,80},{1... | collective-permute-start | bytes 589832 | tf_op jit(solution)/shard_map/ppermute | solution.py:171
  21.4 6.8 %collective-permute-done.5 = f32[96,512]{1,0:T(8,128)S(1)} collective-permute-done((f32[96,512]{1,0:T(8,128)S(1)}, f32[96,512]{1,0:T(8,128)S(1)}, u32[]{:S(2)}, u32[]{:S(2)}) %collective-permute-start.5) | collective-permute-done | bytes 196640 | tf_op jit(solution)/shard_map/ppermute | solution.py:171
  28.2 0.1 collective-permute-start.6
  28.3 2.7 %collective-permute-start.10 = (f32[96,256]{1,0:T(8,128)S(1)}, f32[96,256]{1,0:T(8,128)S(1)}, u32[]{:S(2)}, u32[]{:S(2)}) collective-permute-start(f32[96,256]{1,0:T(8,128)S(1)} %get-tuple-element.31), channel_id=1, source_target_pairs={{0,192},{16,208},{32,224},{48,240},{64,0},{80,16},{96,32},{112,48}... | collective-permute-start | bytes 294920 | tf_op jit(solution)/shard_map/ppermute | solution.py:171
  31.0 1.4 %collective-permute-done.3 = f32[96,512]{1,0:T(8,128)S(1)} collective-permute-done((f32[96,512]{1,0:T(8,128)S(1)}, f32[96,512]{1,0:T(8,128)S(1)}, u32[]{:S(2)}, u32[]{:S(2)}) %collective-permute-start.3) | collective-permute-done | bytes 196640 | tf_op jit(solution)/shard_map/ppermute | solution.py:171
  32.4 4.2 %collective-permute-done.9 = f32[96,512]{1,0:T(8,128)S(1)} collective-permute-done((f32[96,512]{1,0:T(8,128)S(1)}, f32[96,512]{1,0:T(8,128)S(1)}, u32[]{:S(2)}, u32[]{:S(2)}) %collective-permute-start.9) | collective-permute-done | bytes 196640 | tf_op jit(solution)/shard_map/ppermute | solution.py:171
  36.7 0.1 collective-permute-start.7
  36.9 2.7 %collective-permute-start.11 = (f32[96,512]{1,0:T(8,128)S(1)}, f32[96,512]{1,0:T(8,128)S(1)}, u32[]{:S(2)}, u32[]{:S(2)}) collective-permute-start(f32[96,512]{1,0:T(8,128)S(1)} %pad_maximum_fusion.1), channel_id=1, source_target_pairs={{0,192},{16,208},{32,224},{48,240},{64,0},{80,16},{96,32},{112,48}... | collective-permute-start | bytes 589832 | tf_op jit(solution)/shard_map/ppermute | solution.py:171
  39.6 3.6 %collective-permute-done.7 = f32[96,512]{1,0:T(8,128)S(1)} collective-permute-done((f32[96,512]{1,0:T(8,128)S(1)}, f32[96,512]{1,0:T(8,128)S(1)}, u32[]{:S(2)}, u32[]{:S(2)}) %collective-permute-start.7) | collective-permute-done | bytes 196640 | tf_op jit(solution)/shard_map/ppermute | solution.py:171
  43.2 0.1 fusion.5
  43.3 7.0 %collective-permute-start.12 = (f32[96,512]{1,0:T(8,128)S(1)}, f32[96,512]{1,0:T(8,128)S(1)}, u32[]{:S(2)}, u32[]{:S(2)}) collective-permute-start(f32[96,512]{1,0:T(8,128)S(1)} %fusion.5), channel_id=1, source_target_pairs={{0,8},{1,24},{2,40},{3,56},{4,64},{5,80},{6,96},{7,112},{8,136},{9... | collective-permute-start | bytes 589832 | tf_op jit(solution)/shard_map/ppermute | solution.py:192
  50.2 0.1 copy.6
  50.3 12.8 %all_to_all.5.pieces = f32[16,32,96]{2,1,0:T(8,128)S(1)} all-to-all(f32[16,32,96]{2,1,0:T(8,128)S(1)} %bitcast.30), channel_id=1, replica_groups=mesh['row'=16,'col'=16] {'row'}, dimensions={0} | all-to-all | bytes 393216 | tf_op jit(solution)/shard_map/all_to_all | solution.py:194
  63.2 0.8 %in_order.1 = (f32[96,512]{1,0:T(8,128)}, f32[32,1536]{1,0:T(8,128)}) custom-call(f32[96,512]{1,0:T(8,128)S(1)} %collective-permute-done.12.panel, f32[16,32,96]{2,1,0:T(8,128)S(1)} %all_to_all.5.pieces), custom_call_target="tpu_custom_call" | custom-call | tf_op jit(solution)/shard_map/in_order/pallas_call | solution.py:211
  (20 shorter events, 0.3 us)
Async XLA Ops:
  0.6 5.2 %copy-start = (s32[16]{0:T(128)S(1)}, s32[16]{0:T(128)}, u32[]{:S(2)}) copy-start(s32[16]{0:T(128)} %counts.5) | copy-start | bytes 196
  8.4 9.3 %collective-permute-start = (f32[2,96,512]{2,1,0:T(8,128)S(1)}, f32[2,96,512]{2,1,0:T(8,128)S(1)}, u32[]{:S(2)}, u32[]{:S(2)}) collective-permute-start(f32[2,96,512]{2,1,0:T(8,128)S(1)} %get-tuple-element.19), channel_id=1, source_target_pairs={{0,16},{16,0},{32,48},{48,32},{64,80},{80,64},{96,112},{112,96},{1... | collective-permute-start | bytes 1179656 | tf_op jit(solution)/shard_map/ppermute | solution.py:171
  11.7 6.2 %collective-permute-start.4 = (f32[2,96,512]{2,1,0:T(8,128)S(1)}, f32[2,96,512]{2,1,0:T(8,128)S(1)}, u32[]{:S(2)}, u32[]{:S(2)}) collective-permute-start(f32[2,96,512]{2,1,0:T(8,128)S(1)} %get-tuple-element.24), channel_id=1, source_target_pairs={{0,16},{16,0},{32,48},{48,32},{64,80},{80,64},{96,112},{112,96},{1... | collective-permute-start | bytes 1179656 | tf_op jit(solution)/shard_map/ppermute | solution.py:171
  14.5 5.1 %collective-permute-start.2 = (f32[2,96,512]{2,1,0:T(8,128)S(1)}, f32[2,96,512]{2,1,0:T(8,128)S(1)}, u32[]{:S(2)}, u32[]{:S(2)}) collective-permute-start(f32[2,96,512]{2,1,0:T(8,128)S(1)} %get-tuple-element.22), channel_id=1, source_target_pairs={{0,16},{16,0},{32,48},{48,32},{64,80},{80,64},{96,112},{112,96},{1... | collective-permute-start | bytes 1179656 | tf_op jit(solution)/shard_map/ppermute | solution.py:171
  17.6 2.2 %collective-permute-start.8 = (f32[2,96,512]{2,1,0:T(8,128)S(1)}, f32[2,96,512]{2,1,0:T(8,128)S(1)}, u32[]{:S(2)}, u32[]{:S(2)}) collective-permute-start(f32[2,96,512]{2,1,0:T(8,128)S(1)} %get-tuple-element.27), channel_id=1, source_target_pairs={{0,16},{16,0},{32,48},{48,32},{64,80},{80,64},{96,112},{112,96},{1... | collective-permute-start | bytes 1179656 | tf_op jit(solution)/shard_map/ppermute | solution.py:171
  17.8 21.8 %collective-permute-start.1 = (f32[96,512]{1,0:T(8,128)S(1)}, f32[96,512]{1,0:T(8,128)S(1)}, u32[]{:S(2)}, u32[]{:S(2)}) collective-permute-start(f32[96,512]{1,0:T(8,128)S(1)} %slice_bitcast_fusion.6), channel_id=1, source_target_pairs={{0,32},{16,48},{32,0},{48,16},{64,96},{80,112},{96,64},{112,80},{1... | collective-permute-start | bytes 589832 | tf_op jit(solution)/shard_map/ppermute | solution.py:171
  18.0 10.2 %collective-permute-start.5 = (f32[96,512]{1,0:T(8,128)S(1)}, f32[96,512]{1,0:T(8,128)S(1)}, u32[]{:S(2)}, u32[]{:S(2)}) collective-permute-start(f32[96,512]{1,0:T(8,128)S(1)} %slice_bitcast_fusion.2), channel_id=1, source_target_pairs={{0,32},{16,48},{32,0},{48,16},{64,96},{80,112},{96,64},{112,80},{1... | collective-permute-start | bytes 589832 | tf_op jit(solution)/shard_map/ppermute | solution.py:171
  19.6 12.8 %collective-permute-start.3 = (f32[96,512]{1,0:T(8,128)S(1)}, f32[96,512]{1,0:T(8,128)S(1)}, u32[]{:S(2)}, u32[]{:S(2)}) collective-permute-start(f32[96,512]{1,0:T(8,128)S(1)} %slice_bitcast_fusion.4), channel_id=1, source_target_pairs={{0,32},{16,48},{32,0},{48,16},{64,96},{80,112},{96,64},{112,80},{1... | collective-permute-start | bytes 589832 | tf_op jit(solution)/shard_map/ppermute | solution.py:171
  19.8 16.8 %collective-permute-start.9 = (f32[96,512]{1,0:T(8,128)S(1)}, f32[96,512]{1,0:T(8,128)S(1)}, u32[]{:S(2)}, u32[]{:S(2)}) collective-permute-start(f32[96,512]{1,0:T(8,128)S(1)} %slice_bitcast_fusion), channel_id=1, source_target_pairs={{0,32},{16,48},{32,0},{48,16},{64,96},{80,112},{96,64},{112,80},{1... | collective-permute-start | bytes 589832 | tf_op jit(solution)/shard_map/ppermute | solution.py:171
  28.2 8.4 %collective-permute-start.6 = (f32[96,256]{1,0:T(8,128)S(1)}, f32[96,256]{1,0:T(8,128)S(1)}, u32[]{:S(2)}, u32[]{:S(2)}) collective-permute-start(f32[96,256]{1,0:T(8,128)S(1)} %get-tuple-element.30), channel_id=1, source_target_pairs={{0,64},{16,80},{32,96},{48,112},{64,128},{80,144},{96,160},{112,17... | collective-permute-start | bytes 294920 | tf_op jit(solution)/shard_map/ppermute | solution.py:171
  28.3 8.5 %collective-permute-start.10 = (f32[96,256]{1,0:T(8,128)S(1)}, f32[96,256]{1,0:T(8,128)S(1)}, u32[]{:S(2)}, u32[]{:S(2)}) collective-permute-start(f32[96,256]{1,0:T(8,128)S(1)} %get-tuple-element.31), channel_id=1, source_target_pairs={{0,192},{16,208},{32,224},{48,240},{64,0},{80,16},{96,32},{112,48}... | collective-permute-start | bytes 294920 | tf_op jit(solution)/shard_map/ppermute | solution.py:171
  36.7 6.5 %collective-permute-start.7 = (f32[96,512]{1,0:T(8,128)S(1)}, f32[96,512]{1,0:T(8,128)S(1)}, u32[]{:S(2)}, u32[]{:S(2)}) collective-permute-start(f32[96,512]{1,0:T(8,128)S(1)} %pad_maximum_fusion), channel_id=1, source_target_pairs={{0,64},{16,80},{32,96},{48,112},{64,128},{80,144},{96,160},{112,17... | collective-permute-start | bytes 589832 | tf_op jit(solution)/shard_map/ppermute | solution.py:171
  36.9 6.3 %collective-permute-start.11 = (f32[96,512]{1,0:T(8,128)S(1)}, f32[96,512]{1,0:T(8,128)S(1)}, u32[]{:S(2)}, u32[]{:S(2)}) collective-permute-start(f32[96,512]{1,0:T(8,128)S(1)} %pad_maximum_fusion.1), channel_id=1, source_target_pairs={{0,192},{16,208},{32,224},{48,240},{64,0},{80,16},{96,32},{112,48}... | collective-permute-start | bytes 589832 | tf_op jit(solution)/shard_map/ppermute | solution.py:171
  43.3 19.9 %collective-permute-start.12 = (f32[96,512]{1,0:T(8,128)S(1)}, f32[96,512]{1,0:T(8,128)S(1)}, u32[]{:S(2)}, u32[]{:S(2)}) collective-permute-start(f32[96,512]{1,0:T(8,128)S(1)} %fusion.5), channel_id=1, source_target_pairs={{0,8},{1,24},{2,40},{3,56},{4,64},{5,80},{6,96},{7,112},{8,136},{9... | collective-permute-start | bytes 589832 | tf_op jit(solution)/shard_map/ppermute | solution.py:192
